TPU v7x, 128 devices: a whole 4x4x4 slice. The times are simulated.
128 devices in a mesh: grp: 16 (over x, y), blk: 8 (over z, core).
Axes of the slice: x: 4, y: 4, z: 4, core: 2. Of those that a mesh axis runs over, the one named last changes fastest.
Arguments:
- visual: bfloat16 [98304, 3584], P(('grp', 'blk')), may hold values from -6 to 6
- text_queries: float32 [4096, 3584], P(('grp', 'blk')), may hold values from -100 to 100
- kv_weight: bfloat16 [3584, 1024], replicated, may hold values from -0.09375 to 0.09375
- placement: int32 [12288, 1], P(('grp', 'blk')), may hold values from 0 to 127; in each aligned block of 96 rows (0 to 95, 96 to 191, ...) at most 2 rows name the same one
Outputs:
- attended: float32 [4096, 3584], P(('grp', 'blk'))
Inputs may be any that keep to these rules, and one draw needn't show every extreme that they name: `placement`: among the 96 blocks of one frame owner at most 2 name the same attention owner, a bound that some block reaches; every attention owner is named by some block.
All inputs are finite; a program needn't handle non-finite values.
Results may differ from a plain program's by a relative error of at most 0.0003.
Values sent between devices are 32-bit elements; how exact they have to be, the bound alone decides.
No kernel may reach another device: no remote copies, remote signals or barrier semaphores. Data moves between devices by JAX's collectives and lax.ppermute only.
A program may use at most 128 MiB of HBM per device.

v0:
```python
import functools
import math

import jax
import jax.numpy as jnp
from jax import lax
from jax.experimental import pallas as pl
from jax.experimental.pallas import tpu as pltpu
from jax.sharding import PartitionSpec as P

HEADS = 28
KV_HEADS = 4
GROUP = HEADS // KV_HEADS
LANES = 128
HALVES = 2
CAPS = (4, 1)
SPARE = 1
BIAS = -(2.0**99)
EMPTY = (1e30, 4e30, 16e30)
LIVE_BELOW = 1e29
ROWS8 = 8
TILE = 1024
PART = 512
DEPTHS = (512, 1024)


def project_and_pack(placement, visual, kv_weight, caps, segments):
    rows, dv = visual.shape
    width = kv_weight.shape[1]
    blocks = placement.shape[0]
    block_rows = rows // blocks
    owners = KV_HEADS * HALVES
    common = caps[0] + caps[1]
    cuts = [0]
    while cuts[-1] < dv:
        cuts.append(min(dv, cuts[-1] + DEPTHS[min(len(cuts) - 1, len(DEPTHS) - 1)]))
    parts = list(zip(cuts[:-1], cuts[1:]))
    few = math.gcd(segments, 4)

    def body(owner_ref, x_hbm, w_hbm, o1, o2, o3, x, w, buf, mark1, mark2, code, table, sems):
        loads = []
        for i, (a, b) in enumerate(parts):
            loads.append(
                (
                    pltpu.make_async_copy(x_hbm.at[:, a:b], x.at[:, a:b], sems.at[2 * i]),
                    pltpu.make_async_copy(w_hbm.at[a:b], w.at[a:b], sems.at[2 * i + 1]),
                )
            )
            for load in loads[-1]:
                load.start()
        sem, sem2 = (sems.at[2 * len(parts) + i] for i in range(2))
        sem1 = sems.at[2 * len(parts) + 2 :]

        segment = lax.shift_right_logical(owner_ref[...], owners.bit_length() - 1)
        segment = segment.astype(jnp.float32)
        shape = (blocks, blocks)
        i = lax.broadcasted_iota(jnp.int32, shape, 0)
        j = lax.broadcasted_iota(jnp.int32, shape, 1)
        column = jnp.broadcast_to(segment, shape)
        line = jnp.sum(jnp.where(i == j, column, 0.0), axis=0, keepdims=True)
        before = jnp.where((column == line) & (i < j), 1.0, 0.0)
        rank = jnp.sum(before, axis=0, keepdims=True)
        top = jnp.max(rank) + 1.0
        rank = rank.astype(jnp.int32)
        half = jnp.bitwise_and(rank, HALVES - 1)
        slot = lax.shift_right_logical(rank, HALVES.bit_length() - 1)
        code[...] = (line.astype(jnp.int32) * HALVES + half) * ROWS8 + slot
        codes = pltpu.make_async_copy(code, table, sem)
        codes.start()
        level = (top > HALVES * common).astype(jnp.int32)
        level = level + (top > HALVES * (common + SPARE)).astype(jnp.int32)
        mark1[...] = jnp.full(mark1.shape, EMPTY[0], jnp.float32)
        mark = jnp.where(level == 0, EMPTY[0], jnp.where(level == 1, EMPTY[1], EMPTY[2]))
        mark2[...] = jnp.broadcast_to(mark.astype(jnp.float32), mark2.shape)
        fills = [pltpu.make_async_copy(mark2, o2.at[:, :, :, 0], sem2)]
        for g in range(0, segments, mark1.shape[0]):
            to = o1.at[g : g + mark1.shape[0], :, :, 0]
            fills.append(pltpu.make_async_copy(mark1, to, sem1.at[g // mark1.shape[0]]))
        for copy in fills:
            copy.start()
        codes.wait()

        for i, (a, b) in enumerate(parts):
            for load in loads[i]:
                load.wait()
            for kind in range(2):
                for h in range(0, KV_HEADS, 2):
                    c = (kind * KV_HEADS + h) * LANES
                    part = jnp.dot(
                        x[:, a:b], w[a:b, c : c + 2 * LANES], preferred_element_type=jnp.float32
                    )
                    for k in range(2):
                        piece = part[:, k * LANES : (k + 1) * LANES]
                        buf[h + k, kind] = piece if i == 0 else buf[h + k, kind] + piece

        for copy in fills:
            copy.wait()

        def send(j, c):
            at = table[0, j]
            slot = at % ROWS8
            half = at // ROWS8 % HALVES
            seg = at // (ROWS8 * HALVES)
            src = buf.at[:, :, pl.ds(pl.multiple_of(j * block_rows, ROWS8), block_rows), :]

            def copy(out, slot):
                rows_at = pl.ds(pl.multiple_of(slot * block_rows, ROWS8), block_rows)
                dst = out.at[seg, :, half, :, rows_at, :]
                pltpu.make_async_copy(src, dst, sem).start()

            @pl.when(slot < caps[0])
            def _():
                copy(o1, slot)

            @pl.when(slot >= caps[0])
            def _():
                @pl.when(level == 0)
                def _():
                    copy(o2, slot - caps[0])

                @pl.when(level > 0)
                def _():
                    copy(o3, slot - caps[0])

            return c

        lax.fori_loop(0, blocks, send, 0, unroll=4)
        pltpu.make_async_copy(buf, buf, sem).wait()

    shapes = [
        pltpu.HBM((segments, KV_HEADS, HALVES, 2, cap * block_rows, LANES), jnp.float32)
        for cap in caps
    ]
    hbm = pl.BlockSpec(memory_space=pltpu.HBM)
    return pl.pallas_call(
        body,
        out_shape=shapes,
        in_specs=[pl.BlockSpec(memory_space=pltpu.VMEM), hbm, hbm],
        out_specs=[hbm for _ in caps],
        scratch_shapes=[
            pltpu.VMEM((rows, dv), jnp.bfloat16),
            pltpu.VMEM((dv, width), jnp.bfloat16),
            pltpu.VMEM((KV_HEADS, 2, rows, LANES), jnp.float32),
            pltpu.VMEM((few, KV_HEADS, HALVES, caps[0] * block_rows, LANES), jnp.float32),
            pltpu.VMEM((segments, KV_HEADS, HALVES, caps[1] * block_rows, LANES), jnp.float32),
            pltpu.VMEM((1, blocks), jnp.int32),
            pltpu.SMEM((1, blocks), jnp.int32),
            pltpu.SemaphoreType.DMA((2 * len(parts) + 2 + segments // few,)),
        ],
        compiler_params=pltpu.CompilerParams(vmem_limit_bytes=40 * 2**20),
        name="project_and_pack",
    )(
        placement,
        pltpu.with_memory_space_constraint(visual, pltpu.HBM),
        pltpu.with_memory_space_constraint(kv_weight, pltpu.HBM),
    )


def attend(state, queries, me, kv, rows, with_mark=False):
    every = queries.shape[0]
    width = queries.shape[1]
    group = width // LANES
    sources, _, slots, _ = kv.shape
    scale = LANES ** (-0.5) * math.log2(math.e)
    take = min(sources, 1 << (TILE // slots).bit_length() - 1)
    while sources % take:
        take //= 2
    keys = take * slots
    part = PART
    while keys % part:
        part //= 2
    steps = sources // take
    first = state is None
    owners = every // rows
    columns = (group + 1) * LANES

    def body(me_ref, *refs):
        refs = list(refs)
        s_ref = None if first else refs.pop(0)
        q_ref, kv_ref, o_ref = refs[:3]
        f_ref = refs[3] if with_mark else None
        q_s, m_s, l_s, acc_s, k_s, v_s = refs[-6:]
        step = pl.program_id(0)

        @pl.when(step == 0)
        def _():
            ones = (lax.broadcasted_iota(jnp.int32, (every, LANES), 1) == 0).astype(jnp.float32)
            ones = ones.astype(jnp.bfloat16)
            me = me_ref[0]
            for p in range(owners):
                core = jnp.bitwise_and(me ^ p, HALVES - 1)
                away = lax.shift_right_logical(me ^ p, HALVES.bit_length() - 1)
                at = pl.multiple_of((core * KV_HEADS + away) * rows, rows)
                to = slice(p * rows, (p + 1) * rows)
                for j in range(group):
                    x = q_ref[pl.ds(at, rows), j * LANES : (j + 1) * LANES] * scale
                    hi = x.astype(jnp.bfloat16)
                    lo = (x - hi.astype(jnp.float32)).astype(jnp.bfloat16)
                    q_s[j, to, 0 * LANES : 1 * LANES] = hi
                    q_s[j, to, 1 * LANES : 2 * LANES] = lo
                    q_s[j, to, 2 * LANES : 3 * LANES] = hi
            for j in range(group):
                q_s[j, :, 3 * LANES : 4 * LANES] = ones
            if first:
                m_s[...] = jnp.full(m_s.shape, BIAS, jnp.float32)
                l_s[...] = jnp.zeros(l_s.shape, jnp.float32)
                acc_s[...] = jnp.zeros(acc_s.shape, jnp.float32)
            else:
                stats = s_ref[:, :, group * LANES :].reshape(every, LANES)
                lane0 = lax.broadcasted_iota(jnp.int32, (every, LANES), 1) == 0
                for j in range(group):
                    acc_s[j] = s_ref[:, :, j * LANES : (j + 1) * LANES].reshape(every, LANES)
                    m_s[j] = jnp.broadcast_to(stats[:, j : j + 1], (every, LANES))
                    total = jnp.broadcast_to(
                        stats[:, LANES // 2 + j : LANES // 2 + j + 1], (every, LANES)
                    )
                    l_s[j] = jnp.where(lane0, total, 0.0)

        live = kv_ref[:, 0] < LIVE_BELOW
        key = jnp.where(live, kv_ref[:, 0], 0.0).reshape(keys, LANES)
        value = jnp.where(live, kv_ref[:, 1], 0.0).reshape(keys, LANES)
        lane = lax.broadcasted_iota(jnp.int32, (take, slots, LANES), 2)
        bias = jnp.where(live | (lane != 0), 0.0, BIAS).reshape(keys, LANES)
        k_hi = key.astype(jnp.bfloat16)
        k_s[:, 0 * LANES : 1 * LANES] = k_hi
        k_s[:, 1 * LANES : 2 * LANES] = k_hi
        k_s[:, 2 * LANES : 3 * LANES] = (key - k_hi.astype(jnp.float32)).astype(jnp.bfloat16)
        k_s[:, 3 * LANES : 4 * LANES] = bias.astype(jnp.bfloat16)
        v_hi = value.astype(jnp.bfloat16)
        v_s[:, :LANES] = v_hi
        v_s[:, LANES:] = (value - v_hi.astype(jnp.float32)).astype(jnp.bfloat16)
        if with_mark:
            mark = jnp.max(jnp.max(kv_ref[:, 0].reshape(keys, LANES), axis=0, keepdims=True))
            mark = jnp.broadcast_to(mark, f_ref.shape)

            @pl.when(step == 0)
            def _():
                f_ref[...] = mark

            @pl.when(step > 0)
            def _():
                f_ref[...] = jnp.maximum(f_ref[...], mark)

        def score(t, j):
            return lax.dot_general(
                q_s[j],
                k_s[t * part : (t + 1) * part],
                (((1,), (1,)), ((), ())),
                preferred_element_type=jnp.float32,
            )

        def weigh(j, scores):
            old = m_s[j]
            fresh = jnp.maximum(old, jnp.max(scores, axis=1, keepdims=True))
            factor = jnp.exp2(old - fresh)
            weights = jnp.exp2(scores - jnp.tile(fresh, (1, part // LANES)))
            sums = weights[:, :LANES]
            for i in range(1, part // LANES):
                sums = sums + weights[:, i * LANES : (i + 1) * LANES]
            l_s[j] = l_s[j] * factor + sums
            m_s[j] = fresh
            w_hi = weights.astype(jnp.bfloat16)
            return factor, w_hi, (weights - w_hi.astype(jnp.float32)).astype(jnp.bfloat16)

        def gather(t, j, factor, w_hi, w_lo):
            at = slice(t * part, (t + 1) * part)
            both = jnp.dot(w_hi, v_s[at], preferred_element_type=jnp.float32)
            rest = jnp.dot(w_lo, v_s[at, :LANES], preferred_element_type=jnp.float32)
            acc_s[j] = acc_s[j] * factor + (both[:, :LANES] + both[:, LANES:] + rest)

        items = [(t, j) for t in range(keys // part) for j in range(group)]
        scores = score(*items[0])
        behind = None
        for n, item in enumerate(items):
            ahead = score(*items[n + 1]) if n + 1 < len(items) else None
            weighed = weigh(item[1], scores)
            if behind is not None:
                gather(*behind)
            behind = (*item, *weighed)
            scores = ahead
        gather(*behind)

        @pl.when(step == steps - 1)
        def _():
            lane = lax.broadcasted_iota(jnp.int32, (every, LANES), 1)
            stats = jnp.zeros((every, LANES), jnp.float32)
            for j in range(group):
                o_ref[:, :, j * LANES : (j + 1) * LANES] = acc_s[j].reshape(owners, rows, LANES)
                total = jnp.sum(l_s[j], axis=1, keepdims=True)
                stats = jnp.where(lane == j, m_s[j], stats)
                stats = jnp.where(lane == LANES // 2 + j, total, stats)
            o_ref[:, :, group * LANES :] = stats.reshape(owners, rows, LANES)

    state_spec = pl.BlockSpec((owners, rows, columns), lambda i, me: (0, 0, 0))
    in_specs = [
        pl.BlockSpec((every, width), lambda i, me: (0, 0)),
        pl.BlockSpec((take, 2, slots, LANES), lambda i, me: (i, 0, 0, 0)),
    ]
    args = (queries, kv)
    if not first:
        in_specs = [state_spec] + in_specs
        args = (state,) + args
    out_shape = [jax.ShapeDtypeStruct((owners, rows, columns), jnp.float32)]
    out_specs = [state_spec]
    if with_mark:
        out_shape.append(jax.ShapeDtypeStruct((ROWS8, LANES), jnp.float32))
        out_specs.append(pl.BlockSpec((ROWS8, LANES), lambda i, me: (0, 0)))
    out = pl.pallas_call(
        body,
        out_shape=out_shape,
        grid_spec=pltpu.PrefetchScalarGridSpec(
            num_scalar_prefetch=1,
            grid=(steps,),
            in_specs=in_specs,
            out_specs=out_specs,
            scratch_shapes=[
                pltpu.VMEM((group, every, 4 * LANES), jnp.bfloat16),
                pltpu.VMEM((group, every, LANES), jnp.float32),
                pltpu.VMEM((group, every, LANES), jnp.float32),
                pltpu.VMEM((group, every, LANES), jnp.float32),
                pltpu.VMEM((keys, 4 * LANES), jnp.bfloat16),
                pltpu.VMEM((keys, 2 * LANES), jnp.bfloat16),
            ],
        ),
        compiler_params=pltpu.CompilerParams(vmem_limit_bytes=50 * 2**20),
        name="attend_first" if first else "attend_more",
    )(me, *args)
    return out if with_mark else out[0]


def combine(parts):
    owners, rows, columns = parts.shape
    group = columns // LANES - 1

    def body(x_ref, o_ref):
        for h in range(owners // HALVES):
            a, b = HALVES * h, HALVES * h + 1
            stats_a = x_ref[a, :, group * LANES :]
            stats_b = x_ref[b, :, group * LANES :]
            peak = jnp.maximum(stats_a, stats_b)
            fa, fb = jnp.exp2(stats_a - peak), jnp.exp2(stats_b - peak)
            total = pltpu.roll(stats_a, LANES // 2, 1) * fa + pltpu.roll(stats_b, LANES // 2, 1) * fb
            fa, fb = fa / total, fb / total
            for j in range(group):
                cols = slice(j * LANES, (j + 1) * LANES)
                out = x_ref[a, :, cols] * fa[:, j : j + 1] + x_ref[b, :, cols] * fb[:, j : j + 1]
                o_ref[:, (h * group + j) * LANES : (h * group + j + 1) * LANES] = out

    return pl.pallas_call(
        body,
        out_shape=jax.ShapeDtypeStruct((rows, owners // HALVES * group * LANES), jnp.float32),
        compiler_params=pltpu.CompilerParams(vmem_limit_bytes=20 * 2**20),
        name="combine",
    )(parts)


def on_device(visual, text_queries, kv_weight, placement):
    axes = ("grp", "blk")
    segments = lax.axis_size("grp")
    owners = lax.axis_size("blk")
    devices = segments * owners
    blocks = placement.shape[0]
    block_rows = visual.shape[0] // blocks
    rows = text_queries.shape[0]
    per_pair = max(2, blocks // devices + 1)
    most = owners * per_pair // HALVES
    caps = CAPS + (most - CAPS[0],)
    common = sum(CAPS)

    owner = placement.reshape(blocks)
    packed = project_and_pack(placement, visual, kv_weight, caps, segments)

    me = lax.axis_index("blk").astype(jnp.int32)
    text, *packed = lax.optimization_barrier((text_queries, *packed))
    width = text.shape[1] // KV_HEADS
    pieces = []
    for away in range(KV_HEADS):
        z = lax.shift_right_logical(me, HALVES.bit_length() - 1) ^ away
        piece = lax.dynamic_slice_in_dim(text, z * width, width, 1)
        if away:
            pairs = [(k, k ^ (away * HALVES)) for k in range(owners)]
            piece = lax.ppermute(piece, "blk", pairs)
        pieces.append(piece)
    own_core = jnp.concatenate(pieces, axis=0)
    other = lax.ppermute(own_core, "blk", [(k, k ^ 1) for k in range(owners)])
    queries = jnp.concatenate([own_core, other], axis=0)
    packed[1], queries = lax.optimization_barrier((packed[1], queries))
    me = me.reshape(1)

    def exchange(chunk):
        chunk = chunk.reshape(devices, 2, -1, LANES)
        return lax.all_to_all(chunk, axes, 0, 0, tiled=True)

    def beyond(slots, state):
        counts = jnp.sum(
            (owner[None, :] // owners == jnp.arange(segments)[:, None]).astype(jnp.int32), axis=1
        )
        mine = jnp.max(counts) > HALVES * common
        half = jnp.arange(HALVES)[None, :]
        held = (counts[:, None] + (HALVES - 1) - half) // HALVES - caps[0]
        held = jnp.where(mine, held, 0)[:, None, :, None, None, None]
        slot = (jnp.arange(slots * block_rows) // block_rows)[:, None]
        chunk = packed[2][:, :, :, :, : slots * block_rows]
        chunk = jnp.where(slot < held, chunk, EMPTY[0])
        return attend(state, queries, me, exchange(chunk), rows)

    first = exchange(packed[0])
    second = exchange(packed[1])
    state = attend(None, queries, me, first, rows)
    state, mark = attend(state, queries, me, second, rows, with_mark=True)
    mark = mark[0, 0]
    level = (mark > 2 * EMPTY[0]).astype(jnp.int32) + (mark > 2 * EMPTY[1]).astype(jnp.int32)
    state = lax.switch(
        level,
        [
            lambda s: s,
            lambda s: beyond(CAPS[1] + SPARE, s),
            lambda s: beyond(caps[2], s),
        ],
        state,
    )
    parts = lax.all_to_all(state, "blk", 0, 0, tiled=True)
    return combine(parts)


def solution(mesh):
    placed = (P(("grp", "blk"), None), P(("grp", "blk"), None), P(), P(("grp", "blk"), None))
    return jax.shard_map(
        on_device, mesh=mesh, in_specs=placed, out_specs=P(("grp", "blk"), None), check_vma=False
    )
```

profile of v0, /device:TPU:1, one launch (start us, length us, event | category | flops | bytes accessed | tf_op | source)
XLA Modules:
  0.0 139.9 jit_solution(4621747044803258322)
XLA Ops:
  0.0 0.8 copy.6.owner_ref
  0.8 12.3 %project_and_pack.1 = (f32[16,4,2,2,32,128]{5,4,3,2,1,0:T(8,128)}, f32[16,4,2,2,8,128]{5,4,3,2,1,0:T(8,128)}, f32[16,4,2,2,32,128]{5,4,3,2,1,0:T(8,128)}) custom-call(s32[96,1]{1,0:T(8,128)S(1)} %copy.6.owner_ref, bf16[768,3584]{1,0:T(8,128)(2,1)} %x_hbm.1, bf16[3584,1024]{1,0:T(8,128)(2,1)} %w_hbm.1), custom_call_target="tpu_custom_call" | custom-call | tf_op jit(solution)/shard_map/project_and_pack/pallas_call | solution.py:135
  13.0 0.0 copy-start.2
  13.0 11.9 %all-to-all-start.2 = ((f32[128,2,32,128]{3,2,1,0:T(8,128)}), f32[128,2,32,128]{3,2,1,0:T(8,128)}, u32[]{:S(2)}, u32[]{:S(2)}) async-start(f32[128,2,32,128]{3,2,1,0:T(8,128)} %bitcast.24), calls=%async_computation.2 | async-start | bytes 8388608 | tf_op jit(solution)/shard_map/all_to_all | solution.py:392
  25.0 0.0 copy-done.2
  25.0 0.1 constant_dynamic-slice_fusion
  25.1 1.6 %collective-permute-start = (f32[32,896]{1,0:T(8,128)S(1)}, f32[32,896]{1,0:T(8,128)S(1)}, u32[]{:S(2)}, u32[]{:S(2)}) collective-permute-start(f32[32,896]{1,0:T(8,128)S(1)} %get-tuple-element.70), channel_id=1, source_target_pairs={{0,2},{1,3},{2,0},{3,1},{4,6},{5,7},{6,4},{7,5},{8,10},{9,11},{10,... | collective-permute-start | bytes 344072 | tf_op jit(solution)/shard_map/ppermute | solution.py:382
  26.7 2.9 %collective-permute-start.1 = (f32[32,896]{1,0:T(8,128)S(1)}, f32[32,896]{1,0:T(8,128)S(1)}, u32[]{:S(2)}, u32[]{:S(2)}) collective-permute-start(f32[32,896]{1,0:T(8,128)S(1)} %get-tuple-element.69), channel_id=1, source_target_pairs={{0,4},{1,5},{2,6},{3,7},{4,0},{5,1},{6,2},{7,3},{8,12},{9,13},{10,... | collective-permute-start | bytes 344072 | tf_op jit(solution)/shard_map/ppermute | solution.py:382
  29.6 0.0 collective-permute-start.2
  29.6 47.0 %collective-permute-done = f32[32,896]{1,0:T(8,128)S(1)} collective-permute-done((f32[32,896]{1,0:T(8,128)S(1)}, f32[32,896]{1,0:T(8,128)S(1)}, u32[]{:S(2)}, u32[]{:S(2)}) %collective-permute-start) | collective-permute-done | bytes 114720 | tf_op jit(solution)/shard_map/ppermute | solution.py:382
  76.6 1.8 %collective-permute-done.1 = f32[32,896]{1,0:T(8,128)S(1)} collective-permute-done((f32[32,896]{1,0:T(8,128)S(1)}, f32[32,896]{1,0:T(8,128)S(1)}, u32[]{:S(2)}, u32[]{:S(2)}) %collective-permute-start.1) | collective-permute-done | bytes 114720 | tf_op jit(solution)/shard_map/ppermute | solution.py:382
  78.4 0.0 collective-permute-done.2
  78.4 1.4 collective-permute-start.3
  79.9 1.4 collective-permute-done.3
  81.3 0.0 all-to-all-done.2.refs_1_
  81.3 8.6 %all-to-all-start.3 = ((f32[128,2,8,128]{3,2,1,0:T(8,128)}), f32[128,2,8,128]{3,2,1,0:T(8,128)S(1)}, u32[]{:S(2)}, u32[]{:S(2)}) async-start(f32[128,2,8,128]{3,2,1,0:T(8,128)} %bitcast.6), calls=%async_computation.3 | async-start | bytes 2097152 | tf_op jit(solution)/shard_map/all_to_all | solution.py:392
  89.9 0.0 copy-start.3
  89.9 19.9 %attend_first.1.refs_0_ = f32[8,32,1024]{2,1,0:T(8,128)S(1)} custom-call(s32[1]{0:T(128)} %bitcast.4.me_ref, f32[256,896]{1,0:T(8,128)S(1)} %constant_dynamic-update-slice_fusion.refs_0_.refs_1_, f32[128,2,32,128]{3,2,1,0:T(8,128)} %all-to-all-done.2.refs_1_), custom_call_target="tpu_custom_call" | custom-call | tf_op jit(solution)/shard_map/attend_first/pallas_call | solution.py:308
  109.7 0.0 all-to-all-done.3.refs_2_
  109.7 6.0 %attend_more.5 = (f32[8,32,1024]{2,1,0:T(8,128)}, f32[8,128]{1,0:T(8,128)S(1)}) custom-call(s32[1]{0:T(128)} %bitcast.4.me_ref, f32[8,32,1024]{2,1,0:T(8,128)S(1)} %attend_first.1.refs_0_, f32[256,896]{1,0:T(8,128)S(1)} %constant_dynamic-update-slice_fusion.refs_0_.refs_1_, f32[128,2,8,128]{3,2,1,0:T(8,128)S(1)} %all-to-all-done.3.refs_2_), custom_call_target="tpu_custom_call" | custom-call | tf_op jit(solution)/shard_map/attend_more/pallas_call | solution.py:308
  115.8 0.6 slice.6
  117.8 0.0 copy-done.3
  117.8 0.3 conditional.1
  118.1 20.3 %all_to_all.23.x_ref = f32[8,32,1024]{2,1,0:T(8,128)S(1)} all-to-all(f32[8,32,1024]{2,1,0:T(8,128)} %get-tuple-element.73), channel_id=1, replica_groups=mesh['grp'=16,'blk'=8] {'blk'}, dimensions={0} | all-to-all | bytes 2097152 | tf_op jit(solution)/shard_map/all_to_all | solution.py:422
  138.4 1.6 %combine.1 = f32[32,3584]{1,0:T(8,128)} custom-call(f32[8,32,1024]{2,1,0:T(8,128)S(1)} %all_to_all.23.x_ref), custom_call_target="tpu_custom_call" | custom-call | tf_op jit(solution)/shard_map/combine/pallas_call | solution.py:349
  (5 shorter events, 0.1 us)
Async XLA Ops:
  13.0 12.0 %copy-start.2 = (f32[32,3584]{1,0:T(8,128)S(1)}, f32[32,3584]{1,0:T(8,128)}, u32[]{:S(2)}) copy-start(f32[32,3584]{1,0:T(8,128)} %param.8) | copy-start | bytes 1376260
  13.0 68.3 %all-to-all-start.2 = ((f32[128,2,32,128]{3,2,1,0:T(8,128)}), f32[128,2,32,128]{3,2,1,0:T(8,128)}, u32[]{:S(2)}, u32[]{:S(2)}) async-start(f32[128,2,32,128]{3,2,1,0:T(8,128)} %bitcast.24), calls=%async_computation.2 | async-start | bytes 8388608 | tf_op jit(solution)/shard_map/all_to_all | solution.py:392
  25.1 51.5 %collective-permute-start = (f32[32,896]{1,0:T(8,128)S(1)}, f32[32,896]{1,0:T(8,128)S(1)}, u32[]{:S(2)}, u32[]{:S(2)}) collective-permute-start(f32[32,896]{1,0:T(8,128)S(1)} %get-tuple-element.70), channel_id=1, source_target_pairs={{0,2},{1,3},{2,0},{3,1},{4,6},{5,7},{6,4},{7,5},{8,10},{9,11},{10,... | collective-permute-start | bytes 344072 | tf_op jit(solution)/shard_map/ppermute | solution.py:382
  26.7 51.7 %collective-permute-start.1 = (f32[32,896]{1,0:T(8,128)S(1)}, f32[32,896]{1,0:T(8,128)S(1)}, u32[]{:S(2)}, u32[]{:S(2)}) collective-permute-start(f32[32,896]{1,0:T(8,128)S(1)} %get-tuple-element.69), channel_id=1, source_target_pairs={{0,4},{1,5},{2,6},{3,7},{4,0},{5,1},{6,2},{7,3},{8,12},{9,13},{10,... | collective-permute-start | bytes 344072 | tf_op jit(solution)/shard_map/ppermute | solution.py:382
  29.6 48.8 %collective-permute-start.2 = (f32[32,896]{1,0:T(8,128)S(1)}, f32[32,896]{1,0:T(8,128)S(1)}, u32[]{:S(2)}, u32[]{:S(2)}) collective-permute-start(f32[32,896]{1,0:T(8,128)S(1)} %get-tuple-element.68), channel_id=1, source_target_pairs={{0,6},{1,7},{2,4},{3,5},{4,2},{5,3},{6,0},{7,1},{8,14},{9,15},{10,... | collective-permute-start | bytes 344072 | tf_op jit(solution)/shard_map/ppermute | solution.py:382
  78.4 2.8 %collective-permute-start.3 = (f32[128,896]{1,0:T(8,128)S(1)}, f32[128,896]{1,0:T(8,128)S(1)}, u32[]{:S(2)}, u32[]{:S(2)}) collective-permute-start(f32[128,896]{1,0:T(8,128)S(1)} %pad_maximum_fusion), channel_id=1, source_target_pairs={{0,1},{1,0},{2,3},{3,2},{4,5},{5,4},{6,7},{7,6},{8,9},{9,8},{10,11... | collective-permute-start | bytes 1376264 | tf_op jit(solution)/shard_map/ppermute | solution.py:385
  81.3 28.4 %all-to-all-start.3 = ((f32[128,2,8,128]{3,2,1,0:T(8,128)}), f32[128,2,8,128]{3,2,1,0:T(8,128)S(1)}, u32[]{:S(2)}, u32[]{:S(2)}) async-start(f32[128,2,8,128]{3,2,1,0:T(8,128)} %bitcast.6), calls=%async_computation.3 | async-start | bytes 2097152 | tf_op jit(solution)/shard_map/all_to_all | solution.py:392
  89.9 27.9 %copy-start.3 = (s32[96,1]{0,1:T(1,128)S(1)}, s32[96,1]{0,1:T(1,128)}, u32[]{:S(2)}) copy-start(s32[96,1]{0,1:T(1,128)} %param.10) | copy-start | bytes 1156
where the time goes:
time: 140 us
  waiting for transfers between devices  50.2 us (36%)
  Pallas kernels  39.7 us (28%)
  starting transfers between devices  26.4 us (19%)
  blocking collectives  20.3 us (14%)
  between operations  1.54 us (1%)
  local copies, waits for them, and re-layouts  1.48 us (1%)
    ppermute x3, waiting for transfers between devices, on_device(): piece = lax.ppermute(piece, 'blk', pairs)  48.8 us
    pallas_call x2, Pallas kernels, attend(): pl.pallas_call(body, out_shape=out_shape, grid_spec=pltpu.PrefetchScalarG...  25.9 us
    all_to_all x2, starting transfers between devices, exchange(): return lax.all_to_all(chunk, axes, 0, 0, tiled=True)  20.5 us
    all_to_all x1, blocking collectives, on_device(): parts = lax.all_to_all(state, 'blk', 0, 0, tiled=True)  20.3 us
    pallas_call x1, Pallas kernels, project_and_pack(): pl.pallas_call(body, out_shape=shapes, in_specs=[pl.BlockSpec(memory_spac...  12.3 us
    ppermute x3, starting transfers between devices, on_device(): piece = lax.ppermute(piece, 'blk', pairs)  4.52 us
  transfers between devices with their start and end apart: 6, of which 3 were waited for; matrix products, arithmetic and copies ran while one was open for 0% of the time, Pallas kernels for 14%

commit v1 on v0

--- a/solution.py
+++ b/solution.py
@@ -157,8 +157,8 @@
 
 
 def attend(state, queries, me, kv, rows, with_mark=False):
-    every = queries.shape[0]
-    width = queries.shape[1]
+    every = HALVES * queries[0].shape[0]
+    width = queries[0].shape[1]
     group = width // LANES
     sources, _, slots, _ = kv.shape
     scale = LANES ** (-0.5) * math.log2(math.e)
@@ -177,8 +177,8 @@
     def body(me_ref, *refs):
         refs = list(refs)
         s_ref = None if first else refs.pop(0)
-        q_ref, kv_ref, o_ref = refs[:3]
-        f_ref = refs[3] if with_mark else None
+        own_ref, other_ref, kv_ref, o_ref = refs[:4]
+        f_ref = refs[4] if with_mark else None
         q_s, m_s, l_s, acc_s, k_s, v_s = refs[-6:]
         step = pl.program_id(0)
 
@@ -186,14 +186,13 @@
         def _():
             ones = (lax.broadcasted_iota(jnp.int32, (every, LANES), 1) == 0).astype(jnp.float32)
             ones = ones.astype(jnp.bfloat16)
-            me = me_ref[0]
+            core = jnp.bitwise_and(me_ref[0], HALVES - 1)
             for p in range(owners):
-                core = jnp.bitwise_and(me ^ p, HALVES - 1)
-                away = lax.shift_right_logical(me ^ p, HALVES.bit_length() - 1)
-                at = pl.multiple_of((core * KV_HEADS + away) * rows, rows)
+                at = slice(p // HALVES * rows, (p // HALVES + 1) * rows)
                 to = slice(p * rows, (p + 1) * rows)
                 for j in range(group):
-                    x = q_ref[pl.ds(at, rows), j * LANES : (j + 1) * LANES] * scale
+                    cols = slice(j * LANES, (j + 1) * LANES)
+                    x = jnp.where(core == p % HALVES, own_ref[at, cols], other_ref[at, cols]) * scale
                     hi = x.astype(jnp.bfloat16)
                     lo = (x - hi.astype(jnp.float32)).astype(jnp.bfloat16)
                     q_s[j, to, 0 * LANES : 1 * LANES] = hi
@@ -293,10 +292,11 @@
 
     state_spec = pl.BlockSpec((owners, rows, columns), lambda i, me: (0, 0, 0))
     in_specs = [
-        pl.BlockSpec((every, width), lambda i, me: (0, 0)),
+        pl.BlockSpec((every // HALVES, width), lambda i, me: (0, 0)),
+        pl.BlockSpec((every // HALVES, width), lambda i, me: (0, 0)),
         pl.BlockSpec((take, 2, slots, LANES), lambda i, me: (i, 0, 0, 0)),
     ]
-    args = (queries, kv)
+    args = (*queries, kv)
     if not first:
         in_specs = [state_spec] + in_specs
         args = (state,) + args
@@ -368,24 +368,16 @@
     common = sum(CAPS)
 
     owner = placement.reshape(blocks)
-    packed = project_and_pack(placement, visual, kv_weight, caps, segments)
-
-    me = lax.axis_index("blk").astype(jnp.int32)
-    text, *packed = lax.optimization_barrier((text_queries, *packed))
-    width = text.shape[1] // KV_HEADS
-    pieces = []
-    for away in range(KV_HEADS):
-        z = lax.shift_right_logical(me, HALVES.bit_length() - 1) ^ away
-        piece = lax.dynamic_slice_in_dim(text, z * width, width, 1)
-        if away:
-            pairs = [(k, k ^ (away * HALVES)) for k in range(owners)]
-            piece = lax.ppermute(piece, "blk", pairs)
-        pieces.append(piece)
-    own_core = jnp.concatenate(pieces, axis=0)
+    packed = list(project_and_pack(placement, visual, kv_weight, caps, segments))
+
+    q = text_queries.reshape(rows, KV_HEADS, -1).transpose(1, 0, 2)
+    same_core = [[z * HALVES + c for z in range(KV_HEADS)] for c in range(HALVES)]
+    own_core = lax.all_to_all(q, "blk", 0, 0, axis_index_groups=same_core, tiled=True)
+    own_core = own_core.reshape(KV_HEADS * rows, -1)
     other = lax.ppermute(own_core, "blk", [(k, k ^ 1) for k in range(owners)])
-    queries = jnp.concatenate([own_core, other], axis=0)
-    packed[1], queries = lax.optimization_barrier((packed[1], queries))
-    me = me.reshape(1)
+    packed[1], other = lax.optimization_barrier((packed[1], other))
+    queries = (own_core, other)
+    me = lax.axis_index("blk").astype(jnp.int32).reshape(1)
 
     def exchange(chunk):
         chunk = chunk.reshape(devices, 2, -1, LANES)

time: 140 us -> 140 us (level)
  starting transfers between devices: 26.4 us -> 22.8 us
  local copies, waits for them, and re-layouts: 1.48 us -> 3.09 us
    all_to_all x2, waiting for transfers between devices: 0.01 us -> 50.1 us  [exchange(): return lax.all_to_all(chunk, axes, 0, 0, tiled=True)]
    ppermute x3 -> x0, waiting for transfers between devices: 48.8 us -> none  [on_device(): piece = lax.ppermute(piece, 'blk', pairs)]
    all_to_all x0 -> x1, starting transfers between devices: none -> 5.86 us  [on_device(): lax.all_to_all(q, 'blk', 0, 0, axis_index_groups=same_core, tiled=True)]
    all_to_all x2, starting transfers between devices: 20.5 us -> 15.7 us  [exchange(): return lax.all_to_all(chunk, axes, 0, 0, tiled=True)]
    ppermute x3 -> x0, starting transfers between devices: 4.52 us -> none  [on_device(): piece = lax.ppermute(piece, 'blk', pairs)]
    reshape x0 -> x1, local copies, waits for them, and re-layouts: none -> 1.82 us  [on_device(): q = text_queries.reshape(rows, KV_HEADS, -1).transpose(1, 0, 2)]
  transfers between devices with their start and end apart: 6 -> 4, of which waited for: 3 -> 2; matrix products, arithmetic and copies ran while one was open for 0% -> 1% of each run, Pallas kernels for 14% -> 23%
where the time goes in v1:
time: 140 us; the launch traced here: 139 us
  waiting for transfers between devices  51.6 us (37%)
  Pallas kernels  39.8 us (28%)
  starting transfers between devices  22.8 us (16%)
  blocking collectives  20.3 us (14%)
  local copies, waits for them, and re-layouts  3.09 us (2%)
    all_to_all x2, waiting for transfers between devices, exchange(): return lax.all_to_all(chunk, axes, 0, 0, tiled=True)  50.1 us
    pallas_call x2, Pallas kernels, attend(): pl.pallas_call(body, out_shape=out_shape, grid_spec=pltpu.PrefetchScalarG...  25.9 us
    all_to_all x1, blocking collectives, on_device(): parts = lax.all_to_all(state, 'blk', 0, 0, tiled=True)  20.3 us
    all_to_all x2, starting transfers between devices, exchange(): return lax.all_to_all(chunk, axes, 0, 0, tiled=True)  15.7 us
    pallas_call x1, Pallas kernels, project_and_pack(): pl.pallas_call(body, out_shape=shapes, in_specs=[pl.BlockSpec(memory_spac...  12.3 us
    all_to_all x1, starting transfers between devices, on_device(): lax.all_to_all(q, 'blk', 0, 0, axis_index_groups=same_core, tiled=True)  5.86 us
  transfers between devices with their start and end apart: 4, of which 2 were waited for; matrix products, arithmetic and copies ran while one was open for 1% of the time, Pallas kernels for 23%

profile of v1, /device:TPU:1, one launch (start us, length us, event | category | flops | bytes accessed | tf_op | source)
XLA Modules:
  0.0 139.1 jit_solution(18433013335660885358)
XLA Ops:
  0.0 1.8 %copy.11 = f32[4,4,8,896]{3,2,0,1:T(8,128)} copy(f32[4,4,8,896]{3,2,1,0:T(8,128)} %bitcast.38) | data formatting | bytes 917504 | tf_op jit(solution)/shard_map/reshape | solution.py:373
  1.8 5.9 %all-to-all-start.2 = ((f32[4,32,896]{2,1,0:T(8,128)}), f32[4,32,896]{2,1,0:T(8,128)S(1)}, u32[]{:S(2)}, u32[]{:S(2)}) async-start(f32[4,32,896]{2,1,0:T(8,128)} %bitcast.29), calls=%async_computation.2 | async-start | bytes 917504 | tf_op jit(solution)/shard_map/all_to_all | solution.py:375
  7.7 0.8 copy.8.owner_ref
  8.4 12.3 %project_and_pack.1 = (f32[16,4,2,2,32,128]{5,4,3,2,1,0:T(8,128)}, f32[16,4,2,2,8,128]{5,4,3,2,1,0:T(8,128)}, f32[16,4,2,2,32,128]{5,4,3,2,1,0:T(8,128)}) custom-call(s32[96,1]{1,0:T(8,128)S(1)} %copy.8.owner_ref, bf16[768,3584]{1,0:T(8,128)(2,1)} %x_hbm.1, bf16[3584,1024]{1,0:T(8,128)(2,1)} %w_hbm.1), custom_call_target="tpu_custom_call" | custom-call | tf_op jit(solution)/shard_map/project_and_pack/pallas_call | solution.py:135
  20.7 0.0 all-to-all-done.2
  20.7 10.9 %all-to-all-start.3 = ((f32[128,2,32,128]{3,2,1,0:T(8,128)}), f32[128,2,32,128]{3,2,1,0:T(8,128)}, u32[]{:S(2)}, u32[]{:S(2)}) async-start(f32[128,2,32,128]{3,2,1,0:T(8,128)} %bitcast.37), calls=%async_computation.3 | async-start | bytes 8388608 | tf_op jit(solution)/shard_map/all_to_all | solution.py:384
  31.6 1.2 collective-permute-start
  32.8 1.4 %collective-permute-done.refs_1_.refs_2_ = f32[128,896]{1,0:T(8,128)S(1)} collective-permute-done((f32[128,896]{1,0:T(8,128)S(1)}, f32[128,896]{1,0:T(8,128)S(1)}, u32[]{:S(2)}, u32[]{:S(2)}) %collective-permute-start) | collective-permute-done | bytes 458784 | tf_op jit(solution)/shard_map/ppermute | solution.py:377
  34.3 50.1 %all-to-all-done.3.refs_2_ = f32[128,2,32,128]{3,2,1,0:T(8,128)} async-done(((f32[128,2,32,128]{3,2,1,0:T(8,128)}), f32[128,2,32,128]{3,2,1,0:T(8,128)}, u32[]{:S(2)}, u32[]{:S(2)}) %all-to-all-start.3) | async-done | bytes 4194336 | tf_op jit(solution)/shard_map/all_to_all | solution.py:384
  84.4 4.8 %all-to-all-start.4 = ((f32[128,2,8,128]{3,2,1,0:T(8,128)}), f32[128,2,8,128]{3,2,1,0:T(8,128)S(1)}, u32[]{:S(2)}, u32[]{:S(2)}) async-start(f32[128,2,8,128]{3,2,1,0:T(8,128)} %bitcast.8), calls=%async_computation.4 | async-start | bytes 2097152 | tf_op jit(solution)/shard_map/all_to_all | solution.py:384
  89.2 0.0 copy-start.3
  89.2 19.9 %attend_first.1.refs_0_ = f32[8,32,1024]{2,1,0:T(8,128)S(1)} custom-call(s32[1]{0:T(128)} %bitcast.4.me_ref, f32[128,896]{1,0:T(8,128)S(1)} %bitcast.32, f32[128,896]{1,0:T(8,128)S(1)} %collective-permute-done.refs_1_.refs_2_, f32[128,2,32,128]{3,2,1,0:T(8,128)} %all-to-all-done.3.refs_2_), custom_call_target="tpu_custom_call" | custom-call | tf_op jit(solution)/shard_map/attend_first/pallas_call | solution.py:308
  109.2 0.0 all-to-all-done.4.refs_3_
  109.2 6.0 %attend_more.5 = (f32[8,32,1024]{2,1,0:T(8,128)}, f32[8,128]{1,0:T(8,128)S(1)}) custom-call(s32[1]{0:T(128)} %bitcast.4.me_ref, f32[8,32,1024]{2,1,0:T(8,128)S(1)} %attend_first.1.refs_0_, f32[128,896]{1,0:T(8,128)S(1)} %bitcast.33, f32[128,896]{1,0:T(8,128)S(1)} %collective-permute-done.refs_1_.refs_2_, f32[128,2,8,128]{3,2,1,0:T(8,128)S(1)} %all-to-all-done.4.refs_3_), custom_call_target="tpu_custom_call" | custom-call | tf_op jit(solution)/shard_map/attend_more/pallas_call | solution.py:308
  115.2 0.5 slice.6
  117.0 0.0 copy-done.3
  117.0 0.3 conditional.1
  117.3 20.3 %all_to_all.28.x_ref = f32[8,32,1024]{2,1,0:T(8,128)S(1)} all-to-all(f32[8,32,1024]{2,1,0:T(8,128)} %get-tuple-element.64), channel_id=1, replica_groups=mesh['grp'=16,'blk'=8] {'blk'}, dimensions={0} | all-to-all | bytes 2097152 | tf_op jit(solution)/shard_map/all_to_all | solution.py:414
  137.6 1.6 %combine.1 = f32[32,3584]{1,0:T(8,128)} custom-call(f32[8,32,1024]{2,1,0:T(8,128)S(1)} %all_to_all.28.x_ref), custom_call_target="tpu_custom_call" | custom-call | tf_op jit(solution)/shard_map/combine/pallas_call | solution.py:349
Async XLA Ops:
  1.8 18.9 %all-to-all-start.2 = ((f32[4,32,896]{2,1,0:T(8,128)}), f32[4,32,896]{2,1,0:T(8,128)S(1)}, u32[]{:S(2)}, u32[]{:S(2)}) async-start(f32[4,32,896]{2,1,0:T(8,128)} %bitcast.29), calls=%async_computation.2 | async-start | bytes 917504 | tf_op jit(solution)/shard_map/all_to_all | solution.py:375
  20.7 63.6 %all-to-all-start.3 = ((f32[128,2,32,128]{3,2,1,0:T(8,128)}), f32[128,2,32,128]{3,2,1,0:T(8,128)}, u32[]{:S(2)}, u32[]{:S(2)}) async-start(f32[128,2,32,128]{3,2,1,0:T(8,128)} %bitcast.37), calls=%async_computation.3 | async-start | bytes 8388608 | tf_op jit(solution)/shard_map/all_to_all | solution.py:384
  31.6 2.7 %collective-permute-start = (f32[128,896]{1,0:T(8,128)S(1)}, f32[128,896]{1,0:T(8,128)S(1)}, u32[]{:S(2)}, u32[]{:S(2)}) collective-permute-start(f32[128,896]{1,0:T(8,128)S(1)} %bitcast.31), channel_id=1, source_target_pairs={{0,1},{1,0},{2,3},{3,2},{4,5},{5,4},{6,7},{7,6},{8,9},{9,8},{10,11... | collective-permute-start | bytes 1376264 | tf_op jit(solution)/shard_map/ppermute | solution.py:377
  84.4 24.8 %all-to-all-start.4 = ((f32[128,2,8,128]{3,2,1,0:T(8,128)}), f32[128,2,8,128]{3,2,1,0:T(8,128)S(1)}, u32[]{:S(2)}, u32[]{:S(2)}) async-start(f32[128,2,8,128]{3,2,1,0:T(8,128)} %bitcast.8), calls=%async_computation.4 | async-start | bytes 2097152 | tf_op jit(solution)/shard_map/all_to_all | solution.py:384
  89.2 27.8 %copy-start.3 = (s32[96,1]{0,1:T(1,128)S(1)}, s32[96,1]{0,1:T(1,128)}, u32[]{:S(2)}) copy-start(s32[96,1]{0,1:T(1,128)} %param.10) | copy-start | bytes 1156

commit v2 on v1

--- a/solution.py
+++ b/solution.py
@@ -27,7 +27,7 @@
 def project_and_pack(placement, visual, kv_weight, caps, segments):
     rows, dv = visual.shape
     width = kv_weight.shape[1]
-    blocks = placement.shape[0]
+    blocks = placement.shape[1]
     block_rows = rows // blocks
     owners = KV_HEADS * HALVES
     common = caps[0] + caps[1]
@@ -52,12 +52,11 @@
         sem1 = sems.at[2 * len(parts) + 2 :]
 
         segment = lax.shift_right_logical(owner_ref[...], owners.bit_length() - 1)
-        segment = segment.astype(jnp.float32)
+        line = segment.astype(jnp.float32)
         shape = (blocks, blocks)
         i = lax.broadcasted_iota(jnp.int32, shape, 0)
         j = lax.broadcasted_iota(jnp.int32, shape, 1)
-        column = jnp.broadcast_to(segment, shape)
-        line = jnp.sum(jnp.where(i == j, column, 0.0), axis=0, keepdims=True)
+        column = jnp.sum(jnp.where(i == j, line, 0.0), axis=1, keepdims=True)
         before = jnp.where((column == line) & (i < j), 1.0, 0.0)
         rank = jnp.sum(before, axis=0, keepdims=True)
         top = jnp.max(rank) + 1.0
@@ -72,9 +71,9 @@
         mark1[...] = jnp.full(mark1.shape, EMPTY[0], jnp.float32)
         mark = jnp.where(level == 0, EMPTY[0], jnp.where(level == 1, EMPTY[1], EMPTY[2]))
         mark2[...] = jnp.broadcast_to(mark.astype(jnp.float32), mark2.shape)
-        fills = [pltpu.make_async_copy(mark2, o2.at[:, :, :, 0], sem2)]
+        fills = [pltpu.make_async_copy(mark2, o2.at[:, :, :, :, :LANES], sem2)]
         for g in range(0, segments, mark1.shape[0]):
-            to = o1.at[g : g + mark1.shape[0], :, :, 0]
+            to = o1.at[g : g + mark1.shape[0], :, :, :, :LANES]
             fills.append(pltpu.make_async_copy(mark1, to, sem1.at[g // mark1.shape[0]]))
         for copy in fills:
             copy.start()
@@ -89,9 +88,10 @@
                     part = jnp.dot(
                         x[:, a:b], w[a:b, c : c + 2 * LANES], preferred_element_type=jnp.float32
                     )
+                    at = slice(kind * LANES, (kind + 1) * LANES)
                     for k in range(2):
                         piece = part[:, k * LANES : (k + 1) * LANES]
-                        buf[h + k, kind] = piece if i == 0 else buf[h + k, kind] + piece
+                        buf[h + k, :, at] = piece if i == 0 else buf[h + k, :, at] + piece
 
         for copy in fills:
             copy.wait()
@@ -101,11 +101,11 @@
             slot = at % ROWS8
             half = at // ROWS8 % HALVES
             seg = at // (ROWS8 * HALVES)
-            src = buf.at[:, :, pl.ds(pl.multiple_of(j * block_rows, ROWS8), block_rows), :]
+            src = buf.at[:, pl.ds(pl.multiple_of(j * block_rows, ROWS8), block_rows), :]
 
             def copy(out, slot):
                 rows_at = pl.ds(pl.multiple_of(slot * block_rows, ROWS8), block_rows)
-                dst = out.at[seg, :, half, :, rows_at, :]
+                dst = out.at[seg, :, half, rows_at, :]
                 pltpu.make_async_copy(src, dst, sem).start()
 
             @pl.when(slot < caps[0])
@@ -128,7 +128,7 @@
         pltpu.make_async_copy(buf, buf, sem).wait()
 
     shapes = [
-        pltpu.HBM((segments, KV_HEADS, HALVES, 2, cap * block_rows, LANES), jnp.float32)
+        pltpu.HBM((segments, KV_HEADS, HALVES, cap * block_rows, 2 * LANES), jnp.float32)
         for cap in caps
     ]
     hbm = pl.BlockSpec(memory_space=pltpu.HBM)
@@ -140,7 +140,7 @@
         scratch_shapes=[
             pltpu.VMEM((rows, dv), jnp.bfloat16),
             pltpu.VMEM((dv, width), jnp.bfloat16),
-            pltpu.VMEM((KV_HEADS, 2, rows, LANES), jnp.float32),
+            pltpu.VMEM((KV_HEADS, rows, 2 * LANES), jnp.float32),
             pltpu.VMEM((few, KV_HEADS, HALVES, caps[0] * block_rows, LANES), jnp.float32),
             pltpu.VMEM((segments, KV_HEADS, HALVES, caps[1] * block_rows, LANES), jnp.float32),
             pltpu.VMEM((1, blocks), jnp.int32),
@@ -156,11 +156,23 @@
     )
 
 
+def split_heads(text):
+    rows, width = text.shape[0], text.shape[1] // KV_HEADS
+
+    def body(x_ref, o_ref):
+        for h in range(KV_HEADS):
+            o_ref[h] = x_ref[:, h * width : (h + 1) * width]
+
+    return pl.pallas_call(
+        body, out_shape=jax.ShapeDtypeStruct((KV_HEADS, rows, width), text.dtype), name="split_heads"
+    )(text)
+
+
 def attend(state, queries, me, kv, rows, with_mark=False):
     every = HALVES * queries[0].shape[0]
     width = queries[0].shape[1]
     group = width // LANES
-    sources, _, slots, _ = kv.shape
+    sources, slots, _ = kv.shape
     scale = LANES ** (-0.5) * math.log2(math.e)
     take = min(sources, 1 << (TILE // slots).bit_length() - 1)
     while sources % take:
@@ -215,9 +227,9 @@
                     )
                     l_s[j] = jnp.where(lane0, total, 0.0)
 
-        live = kv_ref[:, 0] < LIVE_BELOW
-        key = jnp.where(live, kv_ref[:, 0], 0.0).reshape(keys, LANES)
-        value = jnp.where(live, kv_ref[:, 1], 0.0).reshape(keys, LANES)
+        live = kv_ref[:, :, :LANES] < LIVE_BELOW
+        key = jnp.where(live, kv_ref[:, :, :LANES], 0.0).reshape(keys, LANES)
+        value = jnp.where(live, kv_ref[:, :, LANES:], 0.0).reshape(keys, LANES)
         lane = lax.broadcasted_iota(jnp.int32, (take, slots, LANES), 2)
         bias = jnp.where(live | (lane != 0), 0.0, BIAS).reshape(keys, LANES)
         k_hi = key.astype(jnp.bfloat16)
@@ -229,16 +241,17 @@
         v_s[:, :LANES] = v_hi
         v_s[:, LANES:] = (value - v_hi.astype(jnp.float32)).astype(jnp.bfloat16)
         if with_mark:
-            mark = jnp.max(jnp.max(kv_ref[:, 0].reshape(keys, LANES), axis=0, keepdims=True))
-            mark = jnp.broadcast_to(mark, f_ref.shape)
+            mark = jnp.max(jnp.max(kv_ref[:, :, :LANES].reshape(keys, LANES), axis=0, keepdims=True))
+            level = (mark > 2 * EMPTY[0]).astype(jnp.int32)
+            level = level + (mark > 2 * EMPTY[1]).astype(jnp.int32)
 
             @pl.when(step == 0)
             def _():
-                f_ref[...] = mark
+                f_ref[0, 0] = level
 
             @pl.when(step > 0)
             def _():
-                f_ref[...] = jnp.maximum(f_ref[...], mark)
+                f_ref[0, 0] = jnp.maximum(f_ref[0, 0], level)
 
         def score(t, j):
             return lax.dot_general(
@@ -294,7 +307,7 @@
     in_specs = [
         pl.BlockSpec((every // HALVES, width), lambda i, me: (0, 0)),
         pl.BlockSpec((every // HALVES, width), lambda i, me: (0, 0)),
-        pl.BlockSpec((take, 2, slots, LANES), lambda i, me: (i, 0, 0, 0)),
+        pl.BlockSpec((take, slots, 2 * LANES), lambda i, me: (i, 0, 0)),
     ]
     args = (*queries, kv)
     if not first:
@@ -303,8 +316,8 @@
     out_shape = [jax.ShapeDtypeStruct((owners, rows, columns), jnp.float32)]
     out_specs = [state_spec]
     if with_mark:
-        out_shape.append(jax.ShapeDtypeStruct((ROWS8, LANES), jnp.float32))
-        out_specs.append(pl.BlockSpec((ROWS8, LANES), lambda i, me: (0, 0)))
+        out_shape.append(jax.ShapeDtypeStruct((1, 1), jnp.int32))
+        out_specs.append(pl.BlockSpec(memory_space=pltpu.SMEM))
     out = pl.pallas_call(
         body,
         out_shape=out_shape,
@@ -368,9 +381,9 @@
     common = sum(CAPS)
 
     owner = placement.reshape(blocks)
-    packed = list(project_and_pack(placement, visual, kv_weight, caps, segments))
-
-    q = text_queries.reshape(rows, KV_HEADS, -1).transpose(1, 0, 2)
+    packed = list(project_and_pack(owner.reshape(1, blocks), visual, kv_weight, caps, segments))
+
+    q = split_heads(text_queries)
     same_core = [[z * HALVES + c for z in range(KV_HEADS)] for c in range(HALVES)]
     own_core = lax.all_to_all(q, "blk", 0, 0, axis_index_groups=same_core, tiled=True)
     own_core = own_core.reshape(KV_HEADS * rows, -1)
@@ -380,7 +393,7 @@
     me = lax.axis_index("blk").astype(jnp.int32).reshape(1)
 
     def exchange(chunk):
-        chunk = chunk.reshape(devices, 2, -1, LANES)
+        chunk = chunk.reshape(devices, -1, 2 * LANES)
         return lax.all_to_all(chunk, axes, 0, 0, tiled=True)
 
     def beyond(slots, state):
@@ -390,20 +403,18 @@
         mine = jnp.max(counts) > HALVES * common
         half = jnp.arange(HALVES)[None, :]
         held = (counts[:, None] + (HALVES - 1) - half) // HALVES - caps[0]
-        held = jnp.where(mine, held, 0)[:, None, :, None, None, None]
+        held = jnp.where(mine, held, 0)[:, None, :, None, None]
         slot = (jnp.arange(slots * block_rows) // block_rows)[:, None]
-        chunk = packed[2][:, :, :, :, : slots * block_rows]
+        chunk = packed[2][:, :, :, : slots * block_rows]
         chunk = jnp.where(slot < held, chunk, EMPTY[0])
         return attend(state, queries, me, exchange(chunk), rows)
 
     first = exchange(packed[0])
     second = exchange(packed[1])
     state = attend(None, queries, me, first, rows)
-    state, mark = attend(state, queries, me, second, rows, with_mark=True)
-    mark = mark[0, 0]
-    level = (mark > 2 * EMPTY[0]).astype(jnp.int32) + (mark > 2 * EMPTY[1]).astype(jnp.int32)
+    state, level = attend(state, queries, me, second, rows, with_mark=True)
     state = lax.switch(
-        level,
+        level[0, 0],
         [
             lambda s: s,
             lambda s: beyond(CAPS[1] + SPARE, s),

time: 140 us -> 138 us (0.986)
  local copies, waits for them, and re-layouts: 3.09 us -> 0.01 us
  Pallas kernels: 39.8 us -> 41.8 us
    reshape x1 -> x0, local copies, waits for them, and re-layouts: 1.82 us -> none  [on_device(): q = text_queries.reshape(rows, KV_HEADS, -1).transpose(1, 0, 2)]
    pallas_call x0 -> x1, Pallas kernels: none -> 1.81 us  [split_heads(): pl.pallas_call(body, out_shape=jax.ShapeDtypeStruct((KV_HEADS, rows, widt...]
  transfers between devices with their start and end apart: 4 -> 4, of which waited for: 2 -> 2; matrix products, arithmetic and copies ran while one was open for 1% -> 0% of each run, Pallas kernels for 23% -> 24%
where the time goes in v2:
time: 138 us; the launch traced here: 137 us
  waiting for transfers between devices  51.6 us (37%)
  Pallas kernels  41.8 us (30%)
  starting transfers between devices  22.8 us (17%)
  blocking collectives  20.2 us (15%)
    all_to_all x2, waiting for transfers between devices, exchange(): return lax.all_to_all(chunk, axes, 0, 0, tiled=True)  50.1 us
    pallas_call x2, Pallas kernels, attend(): pl.pallas_call(body, out_shape=out_shape, grid_spec=pltpu.PrefetchScalarG...  26 us
    all_to_all x1, blocking collectives, on_device(): parts = lax.all_to_all(state, 'blk', 0, 0, tiled=True)  20.2 us
    all_to_all x2, starting transfers between devices, exchange(): return lax.all_to_all(chunk, axes, 0, 0, tiled=True)  15.8 us
    pallas_call x1, Pallas kernels, project_and_pack(): pl.pallas_call(body, out_shape=shapes, in_specs=[pl.BlockSpec(memory_spac...  12.5 us
    all_to_all x1, starting transfers between devices, on_device(): lax.all_to_all(q, 'blk', 0, 0, axis_index_groups=same_core, tiled=True)  5.86 us
  transfers between devices with their start and end apart: 4, of which 2 were waited for; matrix products, arithmetic and copies ran while one was open for 0% of the time, Pallas kernels for 24%

profile of v2, /device:TPU:1, one launch (start us, length us, event | category | flops | bytes accessed | tf_op | source)
XLA Modules:
  0.0 137.5 jit_solution(14766259069955772777)
XLA Ops:
  0.0 1.8 %split_heads.1 = f32[4,32,896]{2,1,0:T(8,128)} custom-call(f32[32,3584]{1,0:T(8,128)} %x_ref.1), custom_call_target="tpu_custom_call" | custom-call | tf_op jit(solution)/shard_map/split_heads/pallas_call | solution.py:166
  1.8 5.9 %all-to-all-start.2 = ((f32[4,32,896]{2,1,0:T(8,128)}), f32[4,32,896]{2,1,0:T(8,128)S(1)}, u32[]{:S(2)}, u32[]{:S(2)}) async-start(f32[4,32,896]{2,1,0:T(8,128)} %split_heads.1), calls=%async_computation.2 | async-start | bytes 917504 | tf_op jit(solution)/shard_map/all_to_all | solution.py:388
  7.7 12.5 %project_and_pack.1 = (f32[16,4,2,32,256]{4,3,2,1,0:T(8,128)}, f32[16,4,2,8,256]{4,3,2,1,0:T(8,128)}, f32[16,4,2,32,256]{4,3,2,1,0:T(8,128)}) custom-call(s32[1,96]{1,0:T(1,128)} %bitcast.32, bf16[768,3584]{1,0:T(8,128)(2,1)} %x_hbm.1, bf16[3584,1024]{1,0:T(8,128)(2,1)} %w_hbm.1), custom_call_target="tpu_custom_call" | custom-call | tf_op jit(solution)/shard_map/project_and_pack/pallas_call | solution.py:135
  20.2 0.0 all-to-all-done.2
  20.2 10.9 %all-to-all-start.3 = ((f32[128,32,256]{2,1,0:T(8,128)}), f32[128,32,256]{2,1,0:T(8,128)}, u32[]{:S(2)}, u32[]{:S(2)}) async-start(f32[128,32,256]{2,1,0:T(8,128)} %bitcast.31), calls=%async_computation.3 | async-start | bytes 8388608 | tf_op jit(solution)/shard_map/all_to_all | solution.py:397
  31.1 1.2 collective-permute-start
  32.3 1.4 %collective-permute-done.refs_1_.refs_2_ = f32[128,896]{1,0:T(8,128)S(1)} collective-permute-done((f32[128,896]{1,0:T(8,128)S(1)}, f32[128,896]{1,0:T(8,128)S(1)}, u32[]{:S(2)}, u32[]{:S(2)}) %collective-permute-start) | collective-permute-done | bytes 458784 | tf_op jit(solution)/shard_map/ppermute | solution.py:390
  33.8 50.1 %all-to-all-done.3.refs_2_ = f32[128,32,256]{2,1,0:T(8,128)} async-done(((f32[128,32,256]{2,1,0:T(8,128)}), f32[128,32,256]{2,1,0:T(8,128)}, u32[]{:S(2)}, u32[]{:S(2)}) %all-to-all-start.3) | async-done | bytes 4194336 | tf_op jit(solution)/shard_map/all_to_all | solution.py:397
  83.9 4.8 %all-to-all-start.4 = ((f32[128,8,256]{2,1,0:T(8,128)}), f32[128,8,256]{2,1,0:T(8,128)S(1)}, u32[]{:S(2)}, u32[]{:S(2)}) async-start(f32[128,8,256]{2,1,0:T(8,128)} %bitcast.8), calls=%async_computation.4 | async-start | bytes 2097152 | tf_op jit(solution)/shard_map/all_to_all | solution.py:397
  88.7 0.0 copy-start.3
  88.8 20.0 %attend_first.1.refs_0_ = f32[8,32,1024]{2,1,0:T(8,128)S(1)} custom-call(s32[1]{0:T(128)} %bitcast.4.me_ref, f32[128,896]{1,0:T(8,128)S(1)} %bitcast.26, f32[128,896]{1,0:T(8,128)S(1)} %collective-permute-done.refs_1_.refs_2_, f32[128,32,256]{2,1,0:T(8,128)} %all-to-all-done.3.refs_2_), custom_call_target="tpu_custom_call" | custom-call | tf_op jit(solution)/shard_map/attend_first/pallas_call | solution.py:321
  108.7 0.0 all-to-all-done.4.refs_3_
  108.7 6.0 %attend_more.5 = (f32[8,32,1024]{2,1,0:T(8,128)}, s32[1,1]{1,0:T(1,128)}) custom-call(s32[1]{0:T(128)} %bitcast.4.me_ref, f32[8,32,1024]{2,1,0:T(8,128)S(1)} %attend_first.1.refs_0_, f32[128,896]{1,0:T(8,128)S(1)} %bitcast.27, f32[128,896]{1,0:T(8,128)S(1)} %collective-permute-done.refs_1_.refs_2_, f32[128,8,256]{2,1,0:T(8,128)S(1)} %all-to-all-done.4.refs_3_), custom_call_target="tpu_custom_call" | custom-call | tf_op jit(solution)/shard_map/attend_more/pallas_call | solution.py:321
  115.4 0.0 copy-done.3
  115.4 0.3 conditional.1
  115.7 20.2 %all_to_all.28.x_ref = f32[8,32,1024]{2,1,0:T(8,128)S(1)} all-to-all(f32[8,32,1024]{2,1,0:T(8,128)} %get-tuple-element.64), channel_id=1, replica_groups=mesh['grp'=16,'blk'=8] {'blk'}, dimensions={0} | all-to-all | bytes 2097152 | tf_op jit(solution)/shard_map/all_to_all | solution.py:425
  135.9 1.6 %combine.1 = f32[32,3584]{1,0:T(8,128)} custom-call(f32[8,32,1024]{2,1,0:T(8,128)S(1)} %all_to_all.28.x_ref), custom_call_target="tpu_custom_call" | custom-call | tf_op jit(solution)/shard_map/combine/pallas_call | solution.py:362
Async XLA Ops:
  1.8 18.4 %all-to-all-start.2 = ((f32[4,32,896]{2,1,0:T(8,128)}), f32[4,32,896]{2,1,0:T(8,128)S(1)}, u32[]{:S(2)}, u32[]{:S(2)}) async-start(f32[4,32,896]{2,1,0:T(8,128)} %split_heads.1), calls=%async_computation.2 | async-start | bytes 917504 | tf_op jit(solution)/shard_map/all_to_all | solution.py:388
  20.2 63.7 %all-to-all-start.3 = ((f32[128,32,256]{2,1,0:T(8,128)}), f32[128,32,256]{2,1,0:T(8,128)}, u32[]{:S(2)}, u32[]{:S(2)}) async-start(f32[128,32,256]{2,1,0:T(8,128)} %bitcast.31), calls=%async_computation.3 | async-start | bytes 8388608 | tf_op jit(solution)/shard_map/all_to_all | solution.py:397
  31.1 2.7 %collective-permute-start = (f32[128,896]{1,0:T(8,128)S(1)}, f32[128,896]{1,0:T(8,128)S(1)}, u32[]{:S(2)}, u32[]{:S(2)}) collective-permute-start(f32[128,896]{1,0:T(8,128)S(1)} %bitcast.25), channel_id=1, source_target_pairs={{0,1},{1,0},{2,3},{3,2},{4,5},{5,4},{6,7},{7,6},{8,9},{9,8},{10,11... | collective-permute-start | bytes 1376264 | tf_op jit(solution)/shard_map/ppermute | solution.py:390
  83.9 24.8 %all-to-all-start.4 = ((f32[128,8,256]{2,1,0:T(8,128)}), f32[128,8,256]{2,1,0:T(8,128)S(1)}, u32[]{:S(2)}, u32[]{:S(2)}) async-start(f32[128,8,256]{2,1,0:T(8,128)} %bitcast.8), calls=%async_computation.4 | async-start | bytes 2097152 | tf_op jit(solution)/shard_map/all_to_all | solution.py:397
  88.7 26.7 %copy-start.3 = (s32[96,1]{0,1:T(1,128)S(1)}, s32[96,1]{0,1:T(1,128)}, u32[]{:S(2)}) copy-start(s32[96,1]{0,1:T(1,128)} %param.10) | copy-start | bytes 1156

commit v3 on v2

--- a/solution.py
+++ b/solution.py
@@ -13,7 +13,7 @@
 GROUP = HEADS // KV_HEADS
 LANES = 128
 HALVES = 2
-CAPS = (4, 1)
+CAPS = (8, 2)
 SPARE = 1
 BIAS = -(2.0**99)
 EMPTY = (1e30, 4e30, 16e30)
@@ -31,6 +31,7 @@
     block_rows = rows // blocks
     owners = KV_HEADS * HALVES
     common = caps[0] + caps[1]
+    most = caps[0] + caps[2]
     cuts = [0]
     while cuts[-1] < dv:
         cuts.append(min(dv, cuts[-1] + DEPTHS[min(len(cuts) - 1, len(DEPTHS) - 1)]))
@@ -61,19 +62,17 @@
         rank = jnp.sum(before, axis=0, keepdims=True)
         top = jnp.max(rank) + 1.0
         rank = rank.astype(jnp.int32)
-        half = jnp.bitwise_and(rank, HALVES - 1)
-        slot = lax.shift_right_logical(rank, HALVES.bit_length() - 1)
-        code[...] = (line.astype(jnp.int32) * HALVES + half) * ROWS8 + slot
+        code[...] = line.astype(jnp.int32) * most + rank
         codes = pltpu.make_async_copy(code, table, sem)
         codes.start()
-        level = (top > HALVES * common).astype(jnp.int32)
-        level = level + (top > HALVES * (common + SPARE)).astype(jnp.int32)
+        level = (top > common).astype(jnp.int32)
+        level = level + (top > common + SPARE).astype(jnp.int32)
         mark1[...] = jnp.full(mark1.shape, EMPTY[0], jnp.float32)
         mark = jnp.where(level == 0, EMPTY[0], jnp.where(level == 1, EMPTY[1], EMPTY[2]))
         mark2[...] = jnp.broadcast_to(mark.astype(jnp.float32), mark2.shape)
-        fills = [pltpu.make_async_copy(mark2, o2.at[:, :, :, :, :LANES], sem2)]
+        fills = [pltpu.make_async_copy(mark2, o2.at[:, :, :, :LANES], sem2)]
         for g in range(0, segments, mark1.shape[0]):
-            to = o1.at[g : g + mark1.shape[0], :, :, :, :LANES]
+            to = o1.at[g : g + mark1.shape[0], :, :, :LANES]
             fills.append(pltpu.make_async_copy(mark1, to, sem1.at[g // mark1.shape[0]]))
         for copy in fills:
             copy.start()
@@ -98,14 +97,13 @@
 
         def send(j, c):
             at = table[0, j]
-            slot = at % ROWS8
-            half = at // ROWS8 % HALVES
-            seg = at // (ROWS8 * HALVES)
+            slot = at % most
+            seg = at // most
             src = buf.at[:, pl.ds(pl.multiple_of(j * block_rows, ROWS8), block_rows), :]
 
             def copy(out, slot):
                 rows_at = pl.ds(pl.multiple_of(slot * block_rows, ROWS8), block_rows)
-                dst = out.at[seg, :, half, rows_at, :]
+                dst = out.at[seg, :, rows_at, :]
                 pltpu.make_async_copy(src, dst, sem).start()
 
             @pl.when(slot < caps[0])
@@ -128,7 +126,7 @@
         pltpu.make_async_copy(buf, buf, sem).wait()
 
     shapes = [
-        pltpu.HBM((segments, KV_HEADS, HALVES, cap * block_rows, 2 * LANES), jnp.float32)
+        pltpu.HBM((segments, KV_HEADS, cap * block_rows, 2 * LANES), jnp.float32)
         for cap in caps
     ]
     hbm = pl.BlockSpec(memory_space=pltpu.HBM)
@@ -141,8 +139,8 @@
             pltpu.VMEM((rows, dv), jnp.bfloat16),
             pltpu.VMEM((dv, width), jnp.bfloat16),
             pltpu.VMEM((KV_HEADS, rows, 2 * LANES), jnp.float32),
-            pltpu.VMEM((few, KV_HEADS, HALVES, caps[0] * block_rows, LANES), jnp.float32),
-            pltpu.VMEM((segments, KV_HEADS, HALVES, caps[1] * block_rows, LANES), jnp.float32),
+            pltpu.VMEM((few, KV_HEADS, caps[0] * block_rows, LANES), jnp.float32),
+            pltpu.VMEM((segments, KV_HEADS, caps[1] * block_rows, LANES), jnp.float32),
             pltpu.VMEM((1, blocks), jnp.int32),
             pltpu.SMEM((1, blocks), jnp.int32),
             pltpu.SemaphoreType.DMA((2 * len(parts) + 2 + segments // few,)),
@@ -376,7 +374,7 @@
     block_rows = visual.shape[0] // blocks
     rows = text_queries.shape[0]
     per_pair = max(2, blocks // devices + 1)
-    most = owners * per_pair // HALVES
+    most = owners * per_pair
     caps = CAPS + (most - CAPS[0],)
     common = sum(CAPS)
 
@@ -393,19 +391,20 @@
     me = lax.axis_index("blk").astype(jnp.int32).reshape(1)
 
     def exchange(chunk):
-        chunk = chunk.reshape(devices, -1, 2 * LANES)
-        return lax.all_to_all(chunk, axes, 0, 0, tiled=True)
+        groups = [
+            [g * owners + z * HALVES + c for g in range(segments) for z in range(KV_HEADS)]
+            for c in range(HALVES)
+        ]
+        chunk = chunk.reshape(segments * KV_HEADS, -1, 2 * LANES)
+        return lax.all_to_all(chunk, axes, 0, 0, axis_index_groups=groups, tiled=True)
 
     def beyond(slots, state):
         counts = jnp.sum(
             (owner[None, :] // owners == jnp.arange(segments)[:, None]).astype(jnp.int32), axis=1
         )
-        mine = jnp.max(counts) > HALVES * common
-        half = jnp.arange(HALVES)[None, :]
-        held = (counts[:, None] + (HALVES - 1) - half) // HALVES - caps[0]
-        held = jnp.where(mine, held, 0)[:, None, :, None, None]
+        held = jnp.where(jnp.max(counts) > common, counts - caps[0], 0)[:, None, None, None]
         slot = (jnp.arange(slots * block_rows) // block_rows)[:, None]
-        chunk = packed[2][:, :, :, : slots * block_rows]
+        chunk = packed[2][:, :, : slots * block_rows]
         chunk = jnp.where(slot < held, chunk, EMPTY[0])
         return attend(state, queries, me, exchange(chunk), rows)
 

time: 138 us -> 144 us (1.043)
  starting transfers between devices: 22.8 us -> 31.8 us
  waiting for transfers between devices: 51.6 us -> 48 us
  blocking collectives: 20.2 us -> 22.3 us
    all_to_all x2, starting transfers between devices: 15.8 us -> 24.4 us  [exchange(): lax.all_to_all(chunk, axes, 0, 0, axis_index_groups=groups, tiled=True)]
    all_to_all x2, waiting for transfers between devices: 50.1 us -> 46.6 us  [exchange(): lax.all_to_all(chunk, axes, 0, 0, axis_index_groups=groups, tiled=True)]
    all_to_all x1, blocking collectives: 20.2 us -> 22.3 us  [on_device(): parts = lax.all_to_all(state, 'blk', 0, 0, tiled=True)]
  transfers between devices with their start and end apart: 4 -> 4, of which waited for: 2 -> 2; matrix products, arithmetic and copies ran while one was open for 0% -> 0% of each run, Pallas kernels for 24% -> 22%
where the time goes in v3:
time: 144 us
  waiting for transfers between devices  48 us (33%)
  Pallas kernels  41.2 us (29%)
  starting transfers between devices  31.8 us (22%)
  blocking collectives  22.3 us (15%)
    all_to_all x2, waiting for transfers between devices, exchange(): lax.all_to_all(chunk, axes, 0, 0, axis_index_groups=groups, tiled=True)  46.6 us
    pallas_call x2, Pallas kernels, attend(): pl.pallas_call(body, out_shape=out_shape, grid_spec=pltpu.PrefetchScalarG...  25.9 us
    all_to_all x2, starting transfers between devices, exchange(): lax.all_to_all(chunk, axes, 0, 0, axis_index_groups=groups, tiled=True)  24.4 us
    all_to_all x1, blocking collectives, on_device(): parts = lax.all_to_all(state, 'blk', 0, 0, tiled=True)  22.3 us
    pallas_call x1, Pallas kernels, project_and_pack(): pl.pallas_call(body, out_shape=shapes, in_specs=[pl.BlockSpec(memory_spac...  11.9 us
    all_to_all x1, starting transfers between devices, on_device(): lax.all_to_all(q, 'blk', 0, 0, axis_index_groups=same_core, tiled=True)  5.86 us
  transfers between devices with their start and end apart: 4, of which 2 were waited for; matrix products, arithmetic and copies ran while one was open for 0% of the time, Pallas kernels for 22%

profile of v3, /device:TPU:1, one launch (start us, length us, event | category | flops | bytes accessed | tf_op | source)
XLA Modules:
  0.0 144.2 jit_solution(2924047214036186694)
XLA Ops:
  0.0 1.8 %split_heads.1 = f32[4,32,896]{2,1,0:T(8,128)} custom-call(f32[32,3584]{1,0:T(8,128)} %x_ref.1), custom_call_target="tpu_custom_call" | custom-call | tf_op jit(solution)/shard_map/split_heads/pallas_call | solution.py:164
  1.8 5.9 %all-to-all-start.2 = ((f32[4,32,896]{2,1,0:T(8,128)}), f32[4,32,896]{2,1,0:T(8,128)S(1)}, u32[]{:S(2)}, u32[]{:S(2)}) async-start(f32[4,32,896]{2,1,0:T(8,128)} %split_heads.1), calls=%async_computation.2 | async-start | bytes 917504 | tf_op jit(solution)/shard_map/all_to_all | solution.py:386
  7.7 11.9 %project_and_pack.1 = (f32[16,4,64,256]{3,2,1,0:T(8,128)}, f32[16,4,16,256]{3,2,1,0:T(8,128)}, f32[16,4,64,256]{3,2,1,0:T(8,128)}) custom-call(s32[1,96]{1,0:T(1,128)} %bitcast.32, bf16[768,3584]{1,0:T(8,128)(2,1)} %x_hbm.1, bf16[3584,1024]{1,0:T(8,128)(2,1)} %w_hbm.1), custom_call_target="tpu_custom_call" | custom-call | tf_op jit(solution)/shard_map/project_and_pack/pallas_call | solution.py:133
  19.6 0.0 all-to-all-done.2
  19.6 10.7 %all-to-all-start.3 = ((f32[64,64,256]{2,1,0:T(8,128)}), f32[64,64,256]{2,1,0:T(8,128)}, u32[]{:S(2)}, u32[]{:S(2)}) async-start(f32[64,64,256]{2,1,0:T(8,128)} %bitcast.31), calls=%async_computation.3 | async-start | bytes 8388608 | tf_op jit(solution)/shard_map/all_to_all | solution.py:399
  30.3 1.6 %collective-permute-start = (f32[128,896]{1,0:T(8,128)S(1)}, f32[128,896]{1,0:T(8,128)S(1)}, u32[]{:S(2)}, u32[]{:S(2)}) collective-permute-start(f32[128,896]{1,0:T(8,128)S(1)} %bitcast.25), channel_id=1, source_target_pairs={{0,1},{1,0},{2,3},{3,2},{4,5},{5,4},{6,7},{7,6},{8,9},{9,8},{10,11... | collective-permute-start | bytes 1376264 | tf_op jit(solution)/shard_map/ppermute | solution.py:388
  31.8 1.4 %collective-permute-done.refs_1_.refs_2_ = f32[128,896]{1,0:T(8,128)S(1)} collective-permute-done((f32[128,896]{1,0:T(8,128)S(1)}, f32[128,896]{1,0:T(8,128)S(1)}, u32[]{:S(2)}, u32[]{:S(2)}) %collective-permute-start) | collective-permute-done | bytes 458784 | tf_op jit(solution)/shard_map/ppermute | solution.py:388
  33.3 46.6 %all-to-all-done.3.refs_2_ = f32[64,64,256]{2,1,0:T(8,128)} async-done(((f32[64,64,256]{2,1,0:T(8,128)}), f32[64,64,256]{2,1,0:T(8,128)}, u32[]{:S(2)}, u32[]{:S(2)}) %all-to-all-start.3) | async-done | bytes 4194336 | tf_op jit(solution)/shard_map/all_to_all | solution.py:399
  79.8 13.7 %all-to-all-start.4 = ((f32[64,16,256]{2,1,0:T(8,128)}), f32[64,16,256]{2,1,0:T(8,128)S(1)}, u32[]{:S(2)}, u32[]{:S(2)}) async-start(f32[64,16,256]{2,1,0:T(8,128)} %bitcast.8), calls=%async_computation.4 | async-start | bytes 2097152 | tf_op jit(solution)/shard_map/all_to_all | solution.py:399
  93.6 0.0 copy-start.1
  93.6 19.9 %attend_first.1.refs_0_ = f32[8,32,1024]{2,1,0:T(8,128)S(1)} custom-call(s32[1]{0:T(128)} %bitcast.4.me_ref, f32[128,896]{1,0:T(8,128)S(1)} %bitcast.26, f32[128,896]{1,0:T(8,128)S(1)} %collective-permute-done.refs_1_.refs_2_, f32[64,64,256]{2,1,0:T(8,128)} %all-to-all-done.3.refs_2_), custom_call_target="tpu_custom_call" | custom-call | tf_op jit(solution)/shard_map/attend_first/pallas_call | solution.py:319
  113.5 0.0 all-to-all-done.4.refs_3_
  113.5 6.0 %attend_more.5 = (f32[8,32,1024]{2,1,0:T(8,128)}, s32[1,1]{1,0:T(1,128)}) custom-call(s32[1]{0:T(128)} %bitcast.4.me_ref, f32[8,32,1024]{2,1,0:T(8,128)S(1)} %attend_first.1.refs_0_, f32[128,896]{1,0:T(8,128)S(1)} %bitcast.27, f32[128,896]{1,0:T(8,128)S(1)} %collective-permute-done.refs_1_.refs_2_, f32[64,16,256]{2,1,0:T(8,128)S(1)} %all-to-all-done.4.refs_3_), custom_call_target="tpu_custom_call" | custom-call | tf_op jit(solution)/shard_map/attend_more/pallas_call | solution.py:319
  120.2 0.0 copy-done.1
  120.2 0.3 conditional.1
  120.4 22.3 %all_to_all.28.x_ref = f32[8,32,1024]{2,1,0:T(8,128)S(1)} all-to-all(f32[8,32,1024]{2,1,0:T(8,128)} %get-tuple-element.60), channel_id=1, replica_groups=mesh['grp'=16,'blk'=8] {'blk'}, dimensions={0} | all-to-all | bytes 2097152 | tf_op jit(solution)/shard_map/all_to_all | solution.py:424
  142.7 1.6 %combine.1 = f32[32,3584]{1,0:T(8,128)} custom-call(f32[8,32,1024]{2,1,0:T(8,128)S(1)} %all_to_all.28.x_ref), custom_call_target="tpu_custom_call" | custom-call | tf_op jit(solution)/shard_map/combine/pallas_call | solution.py:360
Async XLA Ops:
  1.8 17.8 %all-to-all-start.2 = ((f32[4,32,896]{2,1,0:T(8,128)}), f32[4,32,896]{2,1,0:T(8,128)S(1)}, u32[]{:S(2)}, u32[]{:S(2)}) async-start(f32[4,32,896]{2,1,0:T(8,128)} %split_heads.1), calls=%async_computation.2 | async-start | bytes 917504 | tf_op jit(solution)/shard_map/all_to_all | solution.py:386
  19.6 60.2 %all-to-all-start.3 = ((f32[64,64,256]{2,1,0:T(8,128)}), f32[64,64,256]{2,1,0:T(8,128)}, u32[]{:S(2)}, u32[]{:S(2)}) async-start(f32[64,64,256]{2,1,0:T(8,128)} %bitcast.31), calls=%async_computation.3 | async-start | bytes 8388608 | tf_op jit(solution)/shard_map/all_to_all | solution.py:399
  30.3 3.0 %collective-permute-start = (f32[128,896]{1,0:T(8,128)S(1)}, f32[128,896]{1,0:T(8,128)S(1)}, u32[]{:S(2)}, u32[]{:S(2)}) collective-permute-start(f32[128,896]{1,0:T(8,128)S(1)} %bitcast.25), channel_id=1, source_target_pairs={{0,1},{1,0},{2,3},{3,2},{4,5},{5,4},{6,7},{7,6},{8,9},{9,8},{10,11... | collective-permute-start | bytes 1376264 | tf_op jit(solution)/shard_map/ppermute | solution.py:388
  79.8 33.7 %all-to-all-start.4 = ((f32[64,16,256]{2,1,0:T(8,128)}), f32[64,16,256]{2,1,0:T(8,128)S(1)}, u32[]{:S(2)}, u32[]{:S(2)}) async-start(f32[64,16,256]{2,1,0:T(8,128)} %bitcast.8), calls=%async_computation.4 | async-start | bytes 2097152 | tf_op jit(solution)/shard_map/all_to_all | solution.py:399
  93.6 26.6 %copy-start.1 = (s32[96,1]{0,1:T(1,128)S(1)}, s32[96,1]{0,1:T(1,128)}, u32[]{:S(2)}) copy-start(s32[96,1]{0,1:T(1,128)} %param.10) | copy-start | bytes 1156

commit v4 on v3

--- a/solution.py
+++ b/solution.py
@@ -13,7 +13,7 @@
 GROUP = HEADS // KV_HEADS
 LANES = 128
 HALVES = 2
-CAPS = (8, 2)
+CAPS = (8, 3)
 SPARE = 1
 BIAS = -(2.0**99)
 EMPTY = (1e30, 4e30, 16e30)
@@ -366,9 +366,8 @@
 
 
 def on_device(visual, text_queries, kv_weight, placement):
-    axes = ("grp", "blk")
     segments = lax.axis_size("grp")
-    owners = lax.axis_size("blk")
+    owners = lax.axis_size("z") * lax.axis_size("core")
     devices = segments * owners
     blocks = placement.shape[0]
     block_rows = visual.shape[0] // blocks
@@ -382,21 +381,16 @@
     packed = list(project_and_pack(owner.reshape(1, blocks), visual, kv_weight, caps, segments))
 
     q = split_heads(text_queries)
-    same_core = [[z * HALVES + c for z in range(KV_HEADS)] for c in range(HALVES)]
-    own_core = lax.all_to_all(q, "blk", 0, 0, axis_index_groups=same_core, tiled=True)
+    own_core = lax.all_to_all(q, "z", 0, 0, tiled=True)
     own_core = own_core.reshape(KV_HEADS * rows, -1)
-    other = lax.ppermute(own_core, "blk", [(k, k ^ 1) for k in range(owners)])
+    other = lax.ppermute(own_core, "core", [(k, k ^ 1) for k in range(HALVES)])
     packed[1], other = lax.optimization_barrier((packed[1], other))
     queries = (own_core, other)
-    me = lax.axis_index("blk").astype(jnp.int32).reshape(1)
+    me = lax.axis_index(("z", "core")).astype(jnp.int32).reshape(1)
 
     def exchange(chunk):
-        groups = [
-            [g * owners + z * HALVES + c for g in range(segments) for z in range(KV_HEADS)]
-            for c in range(HALVES)
-        ]
         chunk = chunk.reshape(segments * KV_HEADS, -1, 2 * LANES)
-        return lax.all_to_all(chunk, axes, 0, 0, axis_index_groups=groups, tiled=True)
+        return lax.all_to_all(chunk, ("grp", "z"), 0, 0, tiled=True)
 
     def beyond(slots, state):
         counts = jnp.sum(
@@ -421,12 +415,18 @@
         ],
         state,
     )
-    parts = lax.all_to_all(state, "blk", 0, 0, tiled=True)
+    parts = lax.all_to_all(state, ("z", "core"), 0, 0, tiled=True)
     return combine(parts)
 
 
 def solution(mesh):
-    placed = (P(("grp", "blk"), None), P(("grp", "blk"), None), P(), P(("grp", "blk"), None))
+    shape = (mesh.shape["grp"], mesh.shape["blk"] // HALVES, HALVES)
+    fine = jax.sharding.Mesh(mesh.devices.reshape(shape), ("grp", "z", "core"))
+    every = P(("grp", "z", "core"), None)
     return jax.shard_map(
-        on_device, mesh=mesh, in_specs=placed, out_specs=P(("grp", "blk"), None), check_vma=False
+        on_device,
+        mesh=fine,
+        in_specs=(every, every, P(), every),
+        out_specs=every,
+        check_vma=False,
     )

time: 144 us -> 147 us (1.021)
  Pallas kernels: 41.2 us -> 44.4 us
  starting transfers between devices: 31.8 us -> 29.5 us
    pallas_call x2, Pallas kernels: 25.9 us -> 29 us  [attend(): pl.pallas_call(body, out_shape=out_shape, grid_spec=pltpu.PrefetchScalarG...]
    all_to_all x3, starting transfers between devices: 30.2 us -> 27.8 us  [the longest x2 22 us: exchange(): return lax.all_to_all(chunk, ('grp', 'z'), 0, 0, tiled=True)]
  transfers between devices with their start and end apart: 4 -> 4, of which waited for: 2 -> 3; matrix products, arithmetic and copies ran while one was open for 0% -> 0% of each run, Pallas kernels for 22% -> 22%
where the time goes in v4:
time: 147 us
  waiting for transfers between devices  48.9 us (33%)
  Pallas kernels  44.4 us (30%)
  starting transfers between devices  29.5 us (20%)
  blocking collectives  23 us (16%)
    all_to_all x2, waiting for transfers between devices, exchange(): return lax.all_to_all(chunk, ('grp', 'z'), 0, 0, tiled=True)  47.4 us
    pallas_call x2, Pallas kernels, attend(): pl.pallas_call(body, out_shape=out_shape, grid_spec=pltpu.PrefetchScalarG...  29 us
    all_to_all x1, blocking collectives, on_device(): parts = lax.all_to_all(state, ('z', 'core'), 0, 0, tiled=True)  23 us
    all_to_all x2, starting transfers between devices, exchange(): return lax.all_to_all(chunk, ('grp', 'z'), 0, 0, tiled=True)  22 us
    pallas_call x1, Pallas kernels, project_and_pack(): pl.pallas_call(body, out_shape=shapes, in_specs=[pl.BlockSpec(memory_spac...  12 us
    all_to_all x1, starting transfers between devices, on_device(): own_core = lax.all_to_all(q, 'z', 0, 0, tiled=True)  5.86 us
  transfers between devices with their start and end apart: 4, of which 3 were waited for; matrix products, arithmetic and copies ran while one was open for 0% of the time, Pallas kernels for 22%

profile of v4, /device:TPU:1, one launch (start us, length us, event | category | flops | bytes accessed | tf_op | source)
XLA Modules:
  0.0 146.8 jit_solution(8020757962536961759)
XLA Ops:
  0.0 1.8 %split_heads.1 = f32[4,32,896]{2,1,0:T(8,128)} custom-call(f32[32,3584]{1,0:T(8,128)} %x_ref.1), custom_call_target="tpu_custom_call" | custom-call | tf_op jit(solution)/shard_map/split_heads/pallas_call | solution.py:164
  1.8 5.9 %all-to-all-start.2 = ((f32[4,32,896]{2,1,0:T(8,128)}), f32[4,32,896]{2,1,0:T(8,128)S(1)}, u32[]{:S(2)}, u32[]{:S(2)}) async-start(f32[4,32,896]{2,1,0:T(8,128)} %split_heads.1), calls=%async_computation.2 | async-start | bytes 917504 | tf_op jit(solution)/shard_map/all_to_all | solution.py:384
  7.7 12.0 %project_and_pack.1 = (f32[16,4,64,256]{3,2,1,0:T(8,128)}, f32[16,4,24,256]{3,2,1,0:T(8,128)}, f32[16,4,64,256]{3,2,1,0:T(8,128)}) custom-call(s32[1,96]{1,0:T(1,128)} %bitcast.33, bf16[768,3584]{1,0:T(8,128)(2,1)} %x_hbm.1, bf16[3584,1024]{1,0:T(8,128)(2,1)} %w_hbm.1), custom_call_target="tpu_custom_call" | custom-call | tf_op jit(solution)/shard_map/project_and_pack/pallas_call | solution.py:133
  19.7 0.0 all-to-all-done.2
  19.7 10.6 %all-to-all-start.3 = ((f32[64,64,256]{2,1,0:T(8,128)}), f32[64,64,256]{2,1,0:T(8,128)}, u32[]{:S(2)}, u32[]{:S(2)}) async-start(f32[64,64,256]{2,1,0:T(8,128)} %bitcast.31), calls=%async_computation.3 | async-start | bytes 8388608 | tf_op jit(solution)/shard_map/all_to_all | solution.py:393
  30.3 1.6 %collective-permute-start = (f32[128,896]{1,0:T(8,128)S(1)}, f32[128,896]{1,0:T(8,128)S(1)}, u32[]{:S(2)}, u32[]{:S(2)}) collective-permute-start(f32[128,896]{1,0:T(8,128)S(1)} %bitcast.25), channel_id=1, source_target_pairs={{0,1},{1,0},{2,3},{3,2},{4,5},{5,4},{6,7},{7,6},{8,9},{9,8},{10,11... | collective-permute-start | bytes 1376264 | tf_op jit(solution)/shard_map/ppermute | solution.py:386
  31.9 1.4 collective-permute-done.refs_1_.refs_2_
  33.4 46.9 %all-to-all-done.3.refs_2_ = f32[64,64,256]{2,1,0:T(8,128)} async-done(((f32[64,64,256]{2,1,0:T(8,128)}), f32[64,64,256]{2,1,0:T(8,128)}, u32[]{:S(2)}, u32[]{:S(2)}) %all-to-all-start.3) | async-done | bytes 4194336 | tf_op jit(solution)/shard_map/all_to_all | solution.py:393
  80.2 11.4 %all-to-all-start.4 = ((f32[64,24,256]{2,1,0:T(8,128)}), f32[64,24,256]{2,1,0:T(8,128)S(1)}, u32[]{:S(2)}, u32[]{:S(2)}) async-start(f32[64,24,256]{2,1,0:T(8,128)} %bitcast.32), calls=%async_computation.4 | async-start | bytes 3145728 | tf_op jit(solution)/shard_map/all_to_all | solution.py:393
  91.6 0.0 copy-start.3
  91.6 19.9 %attend_first.1.refs_0_ = f32[8,32,1024]{2,1,0:T(8,128)S(1)} custom-call(s32[1]{0:T(128)} %bitcast.4.me_ref, f32[128,896]{1,0:T(8,128)S(1)} %bitcast.26, f32[128,896]{1,0:T(8,128)S(1)} %collective-permute-done.refs_1_.refs_2_, f32[64,64,256]{2,1,0:T(8,128)} %all-to-all-done.3.refs_2_), custom_call_target="tpu_custom_call" | custom-call | tf_op jit(solution)/shard_map/attend_first/pallas_call | solution.py:319
  111.6 0.6 all-to-all-done.4.refs_3_
  112.1 9.1 %attend_more.5 = (f32[8,32,1024]{2,1,0:T(8,128)}, s32[1,1]{1,0:T(1,128)}) custom-call(s32[1]{0:T(128)} %bitcast.4.me_ref, f32[8,32,1024]{2,1,0:T(8,128)S(1)} %attend_first.1.refs_0_, f32[128,896]{1,0:T(8,128)S(1)} %bitcast.27, f32[128,896]{1,0:T(8,128)S(1)} %collective-permute-done.refs_1_.refs_2_, f32[64,24,256]{2,1,0:T(8,128)S(1)} %all-to-all-done.4.refs_3_), custom_call_target="tpu_custom_call" | custom-call | tf_op jit(solution)/shard_map/attend_more/pallas_call | solution.py:319
  121.9 0.0 copy-done.3
  121.9 0.3 conditional.1
  122.2 23.0 %all_to_all.28.x_ref = f32[8,32,1024]{2,1,0:T(8,128)S(1)} all-to-all(f32[8,32,1024]{2,1,0:T(8,128)} %get-tuple-element.60), channel_id=1, replica_groups=mesh['grp'=16,'z'=4,'core'=2] {'z','core'}, dimensions={0} | all-to-all | bytes 2097152 | tf_op jit(solution)/shard_map/all_to_all | solution.py:418
  145.2 1.6 %combine.1 = f32[32,3584]{1,0:T(8,128)} custom-call(f32[8,32,1024]{2,1,0:T(8,128)S(1)} %all_to_all.28.x_ref), custom_call_target="tpu_custom_call" | custom-call | tf_op jit(solution)/shard_map/combine/pallas_call | solution.py:360
Async XLA Ops:
  1.8 17.9 %all-to-all-start.2 = ((f32[4,32,896]{2,1,0:T(8,128)}), f32[4,32,896]{2,1,0:T(8,128)S(1)}, u32[]{:S(2)}, u32[]{:S(2)}) async-start(f32[4,32,896]{2,1,0:T(8,128)} %split_heads.1), calls=%async_computation.2 | async-start | bytes 917504 | tf_op jit(solution)/shard_map/all_to_all | solution.py:384
  19.7 60.5 %all-to-all-start.3 = ((f32[64,64,256]{2,1,0:T(8,128)}), f32[64,64,256]{2,1,0:T(8,128)}, u32[]{:S(2)}, u32[]{:S(2)}) async-start(f32[64,64,256]{2,1,0:T(8,128)} %bitcast.31), calls=%async_computation.3 | async-start | bytes 8388608 | tf_op jit(solution)/shard_map/all_to_all | solution.py:393
  30.3 3.0 %collective-permute-start = (f32[128,896]{1,0:T(8,128)S(1)}, f32[128,896]{1,0:T(8,128)S(1)}, u32[]{:S(2)}, u32[]{:S(2)}) collective-permute-start(f32[128,896]{1,0:T(8,128)S(1)} %bitcast.25), channel_id=1, source_target_pairs={{0,1},{1,0},{2,3},{3,2},{4,5},{5,4},{6,7},{7,6},{8,9},{9,8},{10,11... | collective-permute-start | bytes 1376264 | tf_op jit(solution)/shard_map/ppermute | solution.py:386
  80.2 31.9 %all-to-all-start.4 = ((f32[64,24,256]{2,1,0:T(8,128)}), f32[64,24,256]{2,1,0:T(8,128)S(1)}, u32[]{:S(2)}, u32[]{:S(2)}) async-start(f32[64,24,256]{2,1,0:T(8,128)} %bitcast.32), calls=%async_computation.4 | async-start | bytes 3145728 | tf_op jit(solution)/shard_map/all_to_all | solution.py:393
  91.6 30.3 %copy-start.3 = (s32[96,1]{0,1:T(1,128)S(1)}, s32[96,1]{0,1:T(1,128)}, u32[]{:S(2)}) copy-start(s32[96,1]{0,1:T(1,128)} %param.10) | copy-start | bytes 1156

commit v5 on v2

--- a/solution.py
+++ b/solution.py
@@ -98,9 +98,9 @@
 
         def send(j, c):
             at = table[0, j]
-            slot = at % ROWS8
-            half = at // ROWS8 % HALVES
-            seg = at // (ROWS8 * HALVES)
+            slot = jnp.bitwise_and(at, ROWS8 - 1)
+            half = jnp.bitwise_and(lax.shift_right_logical(at, 3), HALVES - 1)
+            seg = lax.shift_right_logical(at, 4)
             src = buf.at[:, pl.ds(pl.multiple_of(j * block_rows, ROWS8), block_rows), :]
 
             def copy(out, slot):
@@ -156,18 +156,6 @@
     )
 
 
-def split_heads(text):
-    rows, width = text.shape[0], text.shape[1] // KV_HEADS
-
-    def body(x_ref, o_ref):
-        for h in range(KV_HEADS):
-            o_ref[h] = x_ref[:, h * width : (h + 1) * width]
-
-    return pl.pallas_call(
-        body, out_shape=jax.ShapeDtypeStruct((KV_HEADS, rows, width), text.dtype), name="split_heads"
-    )(text)
-
-
 def attend(state, queries, me, kv, rows, with_mark=False):
     every = HALVES * queries[0].shape[0]
     width = queries[0].shape[1]
@@ -200,7 +188,8 @@
             ones = ones.astype(jnp.bfloat16)
             core = jnp.bitwise_and(me_ref[0], HALVES - 1)
             for p in range(owners):
-                at = slice(p // HALVES * rows, (p // HALVES + 1) * rows)
+                away = lax.shift_right_logical(me_ref[0] ^ p, HALVES.bit_length() - 1)
+                at = pl.ds(pl.multiple_of(away * rows, rows), rows)
                 to = slice(p * rows, (p + 1) * rows)
                 for j in range(group):
                     cols = slice(j * LANES, (j + 1) * LANES)
@@ -383,14 +372,22 @@
     owner = placement.reshape(blocks)
     packed = list(project_and_pack(owner.reshape(1, blocks), visual, kv_weight, caps, segments))
 
-    q = split_heads(text_queries)
-    same_core = [[z * HALVES + c for z in range(KV_HEADS)] for c in range(HALVES)]
-    own_core = lax.all_to_all(q, "blk", 0, 0, axis_index_groups=same_core, tiled=True)
-    own_core = own_core.reshape(KV_HEADS * rows, -1)
+    me = lax.axis_index("blk").astype(jnp.int32)
+    width = text_queries.shape[1] // KV_HEADS
+    pieces = []
+    for away in range(KV_HEADS):
+        z = lax.shift_right_logical(me, HALVES.bit_length() - 1) ^ away
+        piece = lax.dynamic_slice_in_dim(text_queries, z * width, width, 1)
+        if away:
+            pairs = [(k, k ^ (away * HALVES)) for k in range(owners)]
+            piece = lax.ppermute(piece, "blk", pairs)
+        pieces.append(piece)
+    packed[0], *pieces = lax.optimization_barrier((packed[0], *pieces))
+    own_core = jnp.concatenate(pieces, axis=0)
     other = lax.ppermute(own_core, "blk", [(k, k ^ 1) for k in range(owners)])
     packed[1], other = lax.optimization_barrier((packed[1], other))
     queries = (own_core, other)
-    me = lax.axis_index("blk").astype(jnp.int32).reshape(1)
+    me = me.reshape(1)
 
     def exchange(chunk):
         chunk = chunk.reshape(devices, -1, 2 * LANES)

time: 138 us -> 136 us (0.986)
  Pallas kernels: 41.8 us -> 39.2 us
    all_to_all x1 -> x0, starting transfers between devices: 5.86 us -> none  [on_device(): lax.all_to_all(q, 'blk', 0, 0, axis_index_groups=same_core, tiled=True)]
    ppermute x0 -> x3, starting transfers between devices: none -> 5.85 us  [on_device(): piece = lax.ppermute(piece, 'blk', pairs)]
    pallas_call x1 -> x0, Pallas kernels: 1.81 us -> none  [split_heads(): pl.pallas_call(body, out_shape=jax.ShapeDtypeStruct((KV_HEADS, rows, widt...]
  transfers between devices with their start and end apart: 4 -> 6, of which waited for: 2 -> 2; matrix products, arithmetic and copies ran while one was open for 0% -> 0% of each run, Pallas kernels for 24% -> 23%
where the time goes in v5:
time: 136 us
  waiting for transfers between devices  51.5 us (38%)
  Pallas kernels  39.2 us (29%)
  starting transfers between devices  22.8 us (17%)
  blocking collectives  20.3 us (15%)
    all_to_all x2, waiting for transfers between devices, exchange(): return lax.all_to_all(chunk, axes, 0, 0, tiled=True)  50 us
    pallas_call x2, Pallas kernels, attend(): pl.pallas_call(body, out_shape=out_shape, grid_spec=pltpu.PrefetchScalarG...  25.9 us
    all_to_all x1, blocking collectives, on_device(): parts = lax.all_to_all(state, 'blk', 0, 0, tiled=True)  20.3 us
    all_to_all x2, starting transfers between devices, exchange(): return lax.all_to_all(chunk, axes, 0, 0, tiled=True)  15.7 us
    pallas_call x1, Pallas kernels, project_and_pack(): pl.pallas_call(body, out_shape=shapes, in_specs=[pl.BlockSpec(memory_spac...  11.7 us
    ppermute x3, starting transfers between devices, on_device(): piece = lax.ppermute(piece, 'blk', pairs)  5.85 us
  transfers between devices with their start and end apart: 6, of which 2 were waited for; matrix products, arithmetic and copies ran while one was open for 0% of the time, Pallas kernels for 23%

profile of v5, /device:TPU:1, one launch (start us, length us, event | category | flops | bytes accessed | tf_op | source)
XLA Modules:
  0.0 136.0 jit_solution(13276899059074762273)
XLA Ops:
  0.0 1.1 constant_dynamic-slice_fusion
  1.1 2.5 %collective-permute-start = (f32[32,896]{1,0:T(8,128)S(1)}, f32[32,896]{1,0:T(8,128)S(1)}, u32[]{:S(2)}, u32[]{:S(2)}) collective-permute-start(f32[32,896]{1,0:T(8,128)S(1)} %get-tuple-element.75), channel_id=1, source_target_pairs={{0,2},{1,3},{2,0},{3,1},{4,6},{5,7},{6,4},{7,5},{8,10},{9,11},{10,... | collective-permute-start | bytes 344072 | tf_op jit(solution)/shard_map/ppermute | solution.py:383
  3.6 3.3 %collective-permute-start.1 = (f32[32,896]{1,0:T(8,128)S(1)}, f32[32,896]{1,0:T(8,128)S(1)}, u32[]{:S(2)}, u32[]{:S(2)}) collective-permute-start(f32[32,896]{1,0:T(8,128)S(1)} %get-tuple-element.77), channel_id=1, source_target_pairs={{0,4},{1,5},{2,6},{3,7},{4,0},{5,1},{6,2},{7,3},{8,12},{9,13},{10,... | collective-permute-start | bytes 344072 | tf_op jit(solution)/shard_map/ppermute | solution.py:383
  7.0 0.0 collective-permute-start.2
  7.0 11.7 %project_and_pack.1 = (f32[16,4,2,32,256]{4,3,2,1,0:T(8,128)}, f32[16,4,2,8,256]{4,3,2,1,0:T(8,128)}, f32[16,4,2,32,256]{4,3,2,1,0:T(8,128)}) custom-call(s32[1,96]{1,0:T(1,128)} %bitcast.26, bf16[768,3584]{1,0:T(8,128)(2,1)} %x_hbm.1, bf16[3584,1024]{1,0:T(8,128)(2,1)} %w_hbm.1), custom_call_target="tpu_custom_call" | custom-call | tf_op jit(solution)/shard_map/project_and_pack/pallas_call | solution.py:135
  18.7 0.0 collective-permute-done
  18.7 0.0 collective-permute-done.1
  18.7 0.0 collective-permute-done.2
  18.7 10.9 %all-to-all-start.2 = ((f32[128,32,256]{2,1,0:T(8,128)}), f32[128,32,256]{2,1,0:T(8,128)}, u32[]{:S(2)}, u32[]{:S(2)}) async-start(f32[128,32,256]{2,1,0:T(8,128)} %bitcast.25), calls=%async_computation.2 | async-start | bytes 8388608 | tf_op jit(solution)/shard_map/all_to_all | solution.py:394
  29.7 1.2 collective-permute-start.3
  30.9 1.4 %collective-permute-done.3.refs_1_.refs_2_ = f32[128,896]{1,0:T(8,128)S(1)} collective-permute-done((f32[128,896]{1,0:T(8,128)S(1)}, f32[128,896]{1,0:T(8,128)S(1)}, u32[]{:S(2)}, u32[]{:S(2)}) %collective-permute-start.3) | collective-permute-done | bytes 458784 | tf_op jit(solution)/shard_map/ppermute | solution.py:387
  32.4 50.0 %all-to-all-done.2.refs_2_ = f32[128,32,256]{2,1,0:T(8,128)} async-done(((f32[128,32,256]{2,1,0:T(8,128)}), f32[128,32,256]{2,1,0:T(8,128)}, u32[]{:S(2)}, u32[]{:S(2)}) %all-to-all-start.2) | async-done | bytes 4194336 | tf_op jit(solution)/shard_map/all_to_all | solution.py:394
  82.4 4.8 %all-to-all-start.3 = ((f32[128,8,256]{2,1,0:T(8,128)}), f32[128,8,256]{2,1,0:T(8,128)S(1)}, u32[]{:S(2)}, u32[]{:S(2)}) async-start(f32[128,8,256]{2,1,0:T(8,128)} %bitcast.7), calls=%async_computation.3 | async-start | bytes 2097152 | tf_op jit(solution)/shard_map/all_to_all | solution.py:394
  87.3 0.0 copy-start.2
  87.3 19.9 %attend_first.1.refs_0_ = f32[8,32,1024]{2,1,0:T(8,128)S(1)} custom-call(s32[1]{0:T(128)} %bitcast.4.me_ref, f32[128,896]{1,0:T(8,128)S(1)} %constant_dynamic-update-slice_fusion.refs_0_.refs_1_, f32[128,896]{1,0:T(8,128)S(1)} %collective-permute-done.3.refs_1_.refs_2_, f32[128,32,256]{2,1,0:T(8,128)} %all-to-all-done.2.refs_2_), custom_call_target="tpu_custom_call" | custom-call | tf_op jit(solution)/shard_map/attend_first/pallas_call | solution.py:310
  107.2 0.0 all-to-all-done.3.refs_3_
  107.2 6.0 %attend_more.5 = (f32[8,32,1024]{2,1,0:T(8,128)}, s32[1,1]{1,0:T(1,128)}) custom-call(s32[1]{0:T(128)} %bitcast.4.me_ref, f32[8,32,1024]{2,1,0:T(8,128)S(1)} %attend_first.1.refs_0_, f32[128,896]{1,0:T(8,128)S(1)} %constant_dynamic-update-slice_fusion.refs_0_.refs_1_, f32[128,896]{1,0:T(8,128)S(1)} %collective-permute-done.3.refs_1_.refs_2_, ...), custom_call_target="tpu_custom_call" | custom-call | tf_op jit(solution)/shard_map/attend_more/pallas_call | solution.py:310
  113.9 0.0 copy-done.2
  113.9 0.3 conditional.1
  114.2 20.3 %all_to_all.23.x_ref = f32[8,32,1024]{2,1,0:T(8,128)S(1)} all-to-all(f32[8,32,1024]{2,1,0:T(8,128)} %get-tuple-element.78), channel_id=1, replica_groups=mesh['grp'=16,'blk'=8] {'blk'}, dimensions={0} | all-to-all | bytes 2097152 | tf_op jit(solution)/shard_map/all_to_all | solution.py:422
  134.4 1.6 %combine.1 = f32[32,3584]{1,0:T(8,128)} custom-call(f32[8,32,1024]{2,1,0:T(8,128)S(1)} %all_to_all.23.x_ref), custom_call_target="tpu_custom_call" | custom-call | tf_op jit(solution)/shard_map/combine/pallas_call | solution.py:351
  (4 shorter events, 0.0 us)
Async XLA Ops:
  1.1 17.6 %collective-permute-start = (f32[32,896]{1,0:T(8,128)S(1)}, f32[32,896]{1,0:T(8,128)S(1)}, u32[]{:S(2)}, u32[]{:S(2)}) collective-permute-start(f32[32,896]{1,0:T(8,128)S(1)} %get-tuple-element.75), channel_id=1, source_target_pairs={{0,2},{1,3},{2,0},{3,1},{4,6},{5,7},{6,4},{7,5},{8,10},{9,11},{10,... | collective-permute-start | bytes 344072 | tf_op jit(solution)/shard_map/ppermute | solution.py:383
  3.6 15.0 %collective-permute-start.1 = (f32[32,896]{1,0:T(8,128)S(1)}, f32[32,896]{1,0:T(8,128)S(1)}, u32[]{:S(2)}, u32[]{:S(2)}) collective-permute-start(f32[32,896]{1,0:T(8,128)S(1)} %get-tuple-element.77), channel_id=1, source_target_pairs={{0,4},{1,5},{2,6},{3,7},{4,0},{5,1},{6,2},{7,3},{8,12},{9,13},{10,... | collective-permute-start | bytes 344072 | tf_op jit(solution)/shard_map/ppermute | solution.py:383
  7.0 11.8 %collective-permute-start.2 = (f32[32,896]{1,0:T(8,128)S(1)}, f32[32,896]{1,0:T(8,128)S(1)}, u32[]{:S(2)}, u32[]{:S(2)}) collective-permute-start(f32[32,896]{1,0:T(8,128)S(1)} %get-tuple-element.74), channel_id=1, source_target_pairs={{0,6},{1,7},{2,4},{3,5},{4,2},{5,3},{6,0},{7,1},{8,14},{9,15},{10,... | collective-permute-start | bytes 344072 | tf_op jit(solution)/shard_map/ppermute | solution.py:383
  18.7 63.7 %all-to-all-start.2 = ((f32[128,32,256]{2,1,0:T(8,128)}), f32[128,32,256]{2,1,0:T(8,128)}, u32[]{:S(2)}, u32[]{:S(2)}) async-start(f32[128,32,256]{2,1,0:T(8,128)} %bitcast.25), calls=%async_computation.2 | async-start | bytes 8388608 | tf_op jit(solution)/shard_map/all_to_all | solution.py:394
  29.7 2.7 %collective-permute-start.3 = (f32[128,896]{1,0:T(8,128)S(1)}, f32[128,896]{1,0:T(8,128)S(1)}, u32[]{:S(2)}, u32[]{:S(2)}) collective-permute-start(f32[128,896]{1,0:T(8,128)S(1)} %constant_dynamic-update-slice_fusion.refs_0_.refs_1_), channel_id=1, source_target_pairs={{0,1},{1,0},{2,3},{3,2},{4,5},{5,4},{6,7},{7,6},{8,9},{9,8},{10,11... | collective-permute-start | bytes 1376264 | tf_op jit(solution)/shard_map/ppermute | solution.py:387
  82.4 24.8 %all-to-all-start.3 = ((f32[128,8,256]{2,1,0:T(8,128)}), f32[128,8,256]{2,1,0:T(8,128)S(1)}, u32[]{:S(2)}, u32[]{:S(2)}) async-start(f32[128,8,256]{2,1,0:T(8,128)} %bitcast.7), calls=%async_computation.3 | async-start | bytes 2097152 | tf_op jit(solution)/shard_map/all_to_all | solution.py:394
  87.3 26.6 %copy-start.2 = (s32[96,1]{0,1:T(1,128)S(1)}, s32[96,1]{0,1:T(1,128)}, u32[]{:S(2)}) copy-start(s32[96,1]{0,1:T(1,128)} %param.10) | copy-start | bytes 1156

commit v6 on v4

--- a/solution.py
+++ b/solution.py
@@ -19,7 +19,7 @@
 EMPTY = (1e30, 4e30, 16e30)
 LIVE_BELOW = 1e29
 ROWS8 = 8
-TILE = 1024
+TILE = 1536
 PART = 512
 DEPTHS = (512, 1024)
 
@@ -154,18 +154,6 @@
     )
 
 
-def split_heads(text):
-    rows, width = text.shape[0], text.shape[1] // KV_HEADS
-
-    def body(x_ref, o_ref):
-        for h in range(KV_HEADS):
-            o_ref[h] = x_ref[:, h * width : (h + 1) * width]
-
-    return pl.pallas_call(
-        body, out_shape=jax.ShapeDtypeStruct((KV_HEADS, rows, width), text.dtype), name="split_heads"
-    )(text)
-
-
 def attend(state, queries, me, kv, rows, with_mark=False):
     every = HALVES * queries[0].shape[0]
     width = queries[0].shape[1]
@@ -198,7 +186,8 @@
             ones = ones.astype(jnp.bfloat16)
             core = jnp.bitwise_and(me_ref[0], HALVES - 1)
             for p in range(owners):
-                at = slice(p // HALVES * rows, (p // HALVES + 1) * rows)
+                away = lax.shift_right_logical(me_ref[0] ^ p, HALVES.bit_length() - 1)
+                at = pl.ds(pl.multiple_of(away * rows, rows), rows)
                 to = slice(p * rows, (p + 1) * rows)
                 for j in range(group):
                     cols = slice(j * LANES, (j + 1) * LANES)
@@ -380,13 +369,21 @@
     owner = placement.reshape(blocks)
     packed = list(project_and_pack(owner.reshape(1, blocks), visual, kv_weight, caps, segments))
 
-    q = split_heads(text_queries)
-    own_core = lax.all_to_all(q, "z", 0, 0, tiled=True)
-    own_core = own_core.reshape(KV_HEADS * rows, -1)
+    me = lax.axis_index(("z", "core")).astype(jnp.int32)
+    width = text_queries.shape[1] // KV_HEADS
+    pieces = []
+    for away in range(KV_HEADS):
+        z = lax.axis_index("z").astype(jnp.int32) ^ away
+        piece = lax.dynamic_slice_in_dim(text_queries, z * width, width, 1)
+        if away:
+            piece = lax.ppermute(piece, "z", [(k, k ^ away) for k in range(KV_HEADS)])
+        pieces.append(piece)
+    packed[0], *pieces = lax.optimization_barrier((packed[0], *pieces))
+    own_core = jnp.concatenate(pieces, axis=0)
     other = lax.ppermute(own_core, "core", [(k, k ^ 1) for k in range(HALVES)])
     packed[1], other = lax.optimization_barrier((packed[1], other))
     queries = (own_core, other)
-    me = lax.axis_index(("z", "core")).astype(jnp.int32).reshape(1)
+    me = me.reshape(1)
 
     def exchange(chunk):
         chunk = chunk.reshape(segments * KV_HEADS, -1, 2 * LANES)

time: 147 us -> 146 us (level)
  Pallas kernels: 44.4 us -> 41.8 us
  starting transfers between devices: 29.5 us -> 31.4 us
    all_to_all x1 -> x0, starting transfers between devices: 5.86 us -> none  [on_device(): own_core = lax.all_to_all(q, 'z', 0, 0, tiled=True)]
    ppermute x0 -> x3, starting transfers between devices: none -> 5.85 us  [on_device(): piece = lax.ppermute(piece, 'z', [(k, k ^ away) for k in range(KV_HEADS)])]
    pallas_call x1 -> x0, Pallas kernels: 1.81 us -> none  [split_heads(): pl.pallas_call(body, out_shape=jax.ShapeDtypeStruct((KV_HEADS, rows, widt...]
    all_to_all x2, starting transfers between devices: 22 us -> 23.6 us  [exchange(): return lax.all_to_all(chunk, ('grp', 'z'), 0, 0, tiled=True)]
  transfers between devices with their start and end apart: 4 -> 6, of which waited for: 3 -> 3; matrix products, arithmetic and copies ran while one was open for 0% -> 0% of each run, Pallas kernels for 22% -> 22%
where the time goes in v6:
time: 146 us; the launch traced here: 145 us
  waiting for transfers between devices  47.9 us (33%)
  Pallas kernels  41.8 us (29%)
  starting transfers between devices  31.4 us (22%)
  blocking collectives  22.2 us (15%)
    all_to_all x2, waiting for transfers between devices, exchange(): return lax.all_to_all(chunk, ('grp', 'z'), 0, 0, tiled=True)  46.5 us
    pallas_call x2, Pallas kernels, attend(): pl.pallas_call(body, out_shape=out_shape, grid_spec=pltpu.PrefetchScalarG...  28.2 us
    all_to_all x2, starting transfers between devices, exchange(): return lax.all_to_all(chunk, ('grp', 'z'), 0, 0, tiled=True)  23.6 us
    all_to_all x1, blocking collectives, on_device(): parts = lax.all_to_all(state, ('z', 'core'), 0, 0, tiled=True)  22.2 us
    pallas_call x1, Pallas kernels, project_and_pack(): pl.pallas_call(body, out_shape=shapes, in_specs=[pl.BlockSpec(memory_spac...  12 us
    ppermute x3, starting transfers between devices, on_device(): piece = lax.ppermute(piece, 'z', [(k, k ^ away) for k in range(KV_HEADS)])  5.85 us
  transfers between devices with their start and end apart: 6, of which 3 were waited for; matrix products, arithmetic and copies ran while one was open for 0% of the time, Pallas kernels for 22%

profile of v6, /device:TPU:1, one launch (start us, length us, event | category | flops | bytes accessed | tf_op | source)
XLA Modules:
  0.0 145.5 jit_solution(16222138373283111457)
XLA Ops:
  0.0 1.1 constant_dynamic-slice_fusion
  1.1 2.5 %collective-permute-start = (f32[32,896]{1,0:T(8,128)S(1)}, f32[32,896]{1,0:T(8,128)S(1)}, u32[]{:S(2)}, u32[]{:S(2)}) collective-permute-start(f32[32,896]{1,0:T(8,128)S(1)} %get-tuple-element.71), channel_id=1, source_target_pairs={{0,2},{2,0},{4,6},{6,4},{1,3},{3,1},{5,7},{7,5},{8,10},{10,8},{12,... | collective-permute-start | bytes 344072 | tf_op jit(solution)/shard_map/ppermute | solution.py:379
  3.6 3.3 %collective-permute-start.1 = (f32[32,896]{1,0:T(8,128)S(1)}, f32[32,896]{1,0:T(8,128)S(1)}, u32[]{:S(2)}, u32[]{:S(2)}) collective-permute-start(f32[32,896]{1,0:T(8,128)S(1)} %get-tuple-element.73), channel_id=1, source_target_pairs={{0,4},{2,6},{4,0},{6,2},{1,5},{3,7},{5,1},{7,3},{8,12},{10,14},{12... | collective-permute-start | bytes 344072 | tf_op jit(solution)/shard_map/ppermute | solution.py:379
  7.0 0.0 collective-permute-start.2
  7.0 12.0 %project_and_pack.1 = (f32[16,4,64,256]{3,2,1,0:T(8,128)}, f32[16,4,24,256]{3,2,1,0:T(8,128)}, f32[16,4,64,256]{3,2,1,0:T(8,128)}) custom-call(s32[1,96]{1,0:T(1,128)} %bitcast.27, bf16[768,3584]{1,0:T(8,128)(2,1)} %x_hbm.1, bf16[3584,1024]{1,0:T(8,128)(2,1)} %w_hbm.1), custom_call_target="tpu_custom_call" | custom-call | tf_op jit(solution)/shard_map/project_and_pack/pallas_call | solution.py:133
  18.9 0.0 collective-permute-done
  19.0 0.0 collective-permute-done.1
  19.0 0.0 collective-permute-done.2
  19.0 10.3 %all-to-all-start.2 = ((f32[64,64,256]{2,1,0:T(8,128)}), f32[64,64,256]{2,1,0:T(8,128)}, u32[]{:S(2)}, u32[]{:S(2)}) async-start(f32[64,64,256]{2,1,0:T(8,128)} %bitcast.25), calls=%async_computation.2 | async-start | bytes 8388608 | tf_op jit(solution)/shard_map/all_to_all | solution.py:390
  29.4 2.0 %collective-permute-start.3 = (f32[128,896]{1,0:T(8,128)S(1)}, f32[128,896]{1,0:T(8,128)S(1)}, u32[]{:S(2)}, u32[]{:S(2)}) collective-permute-start(f32[128,896]{1,0:T(8,128)S(1)} %constant_dynamic-update-slice_fusion.refs_0_.refs_1_), channel_id=1, source_target_pairs={{0,1},{1,0},{2,3},{3,2},{4,5},{5,4},{6,7},{7,6},{8,9},{9,8},{10,11... | collective-permute-start | bytes 1376264 | tf_op jit(solution)/shard_map/ppermute | solution.py:383
  31.4 1.4 collective-permute-done.3.refs_1_.refs_2_
  32.8 45.1 %all-to-all-done.2.refs_2_ = f32[64,64,256]{2,1,0:T(8,128)} async-done(((f32[64,64,256]{2,1,0:T(8,128)}), f32[64,64,256]{2,1,0:T(8,128)}, u32[]{:S(2)}, u32[]{:S(2)}) %all-to-all-start.2) | async-done | bytes 4194336 | tf_op jit(solution)/shard_map/all_to_all | solution.py:390
  77.9 13.3 %all-to-all-start.3 = ((f32[64,24,256]{2,1,0:T(8,128)}), f32[64,24,256]{2,1,0:T(8,128)S(1)}, u32[]{:S(2)}, u32[]{:S(2)}) async-start(f32[64,24,256]{2,1,0:T(8,128)} %bitcast.26), calls=%async_computation.3 | async-start | bytes 3145728 | tf_op jit(solution)/shard_map/all_to_all | solution.py:390
  91.1 0.0 copy-start.3
  91.2 20.1 %attend_first.1.refs_0_ = f32[8,32,1024]{2,1,0:T(8,128)S(1)} custom-call(s32[1]{0:T(128)} %bitcast.4.me_ref, f32[128,896]{1,0:T(8,128)S(1)} %constant_dynamic-update-slice_fusion.refs_0_.refs_1_, f32[128,896]{1,0:T(8,128)S(1)} %collective-permute-done.3.refs_1_.refs_2_, f32[64,64,256]{2,1,0:T(8,128)} %all-to-all-done.2.refs_2_), custom_call_target="tpu_custom_call" | custom-call | tf_op jit(solution)/shard_map/attend_first/pallas_call | solution.py:308
  111.2 1.4 all-to-all-done.3.refs_3_
  112.7 8.1 %attend_more.5 = (f32[8,32,1024]{2,1,0:T(8,128)}, s32[1,1]{1,0:T(1,128)}) custom-call(s32[1]{0:T(128)} %bitcast.4.me_ref, f32[8,32,1024]{2,1,0:T(8,128)S(1)} %attend_first.1.refs_0_, f32[128,896]{1,0:T(8,128)S(1)} %constant_dynamic-update-slice_fusion.refs_0_.refs_1_, f32[128,896]{1,0:T(8,128)S(1)} %collective-permute-done.3.refs_1_.refs_2_, ...), custom_call_target="tpu_custom_call" | custom-call | tf_op jit(solution)/shard_map/attend_more/pallas_call | solution.py:308
  121.5 0.0 copy-done.3
  121.5 0.3 conditional.1
  121.7 22.2 %all_to_all.23.x_ref = f32[8,32,1024]{2,1,0:T(8,128)S(1)} all-to-all(f32[8,32,1024]{2,1,0:T(8,128)} %get-tuple-element.74), channel_id=1, replica_groups=mesh['grp'=16,'z'=4,'core'=2] {'z','core'}, dimensions={0} | all-to-all | bytes 2097152 | tf_op jit(solution)/shard_map/all_to_all | solution.py:415
  143.9 1.6 %combine.1 = f32[32,3584]{1,0:T(8,128)} custom-call(f32[8,32,1024]{2,1,0:T(8,128)S(1)} %all_to_all.23.x_ref), custom_call_target="tpu_custom_call" | custom-call | tf_op jit(solution)/shard_map/combine/pallas_call | solution.py:349
  (4 shorter events, 0.0 us)
Async XLA Ops:
  1.1 17.8 %collective-permute-start = (f32[32,896]{1,0:T(8,128)S(1)}, f32[32,896]{1,0:T(8,128)S(1)}, u32[]{:S(2)}, u32[]{:S(2)}) collective-permute-start(f32[32,896]{1,0:T(8,128)S(1)} %get-tuple-element.71), channel_id=1, source_target_pairs={{0,2},{2,0},{4,6},{6,4},{1,3},{3,1},{5,7},{7,5},{8,10},{10,8},{12,... | collective-permute-start | bytes 344072 | tf_op jit(solution)/shard_map/ppermute | solution.py:379
  3.6 15.3 %collective-permute-start.1 = (f32[32,896]{1,0:T(8,128)S(1)}, f32[32,896]{1,0:T(8,128)S(1)}, u32[]{:S(2)}, u32[]{:S(2)}) collective-permute-start(f32[32,896]{1,0:T(8,128)S(1)} %get-tuple-element.73), channel_id=1, source_target_pairs={{0,4},{2,6},{4,0},{6,2},{1,5},{3,7},{5,1},{7,3},{8,12},{10,14},{12... | collective-permute-start | bytes 344072 | tf_op jit(solution)/shard_map/ppermute | solution.py:379
  7.0 12.0 %collective-permute-start.2 = (f32[32,896]{1,0:T(8,128)S(1)}, f32[32,896]{1,0:T(8,128)S(1)}, u32[]{:S(2)}, u32[]{:S(2)}) collective-permute-start(f32[32,896]{1,0:T(8,128)S(1)} %get-tuple-element.70), channel_id=1, source_target_pairs={{0,6},{2,4},{4,2},{6,0},{1,7},{3,5},{5,3},{7,1},{8,14},{10,12},{12... | collective-permute-start | bytes 344072 | tf_op jit(solution)/shard_map/ppermute | solution.py:379
  19.0 58.9 %all-to-all-start.2 = ((f32[64,64,256]{2,1,0:T(8,128)}), f32[64,64,256]{2,1,0:T(8,128)}, u32[]{:S(2)}, u32[]{:S(2)}) async-start(f32[64,64,256]{2,1,0:T(8,128)} %bitcast.25), calls=%async_computation.2 | async-start | bytes 8388608 | tf_op jit(solution)/shard_map/all_to_all | solution.py:390
  29.4 3.4 %collective-permute-start.3 = (f32[128,896]{1,0:T(8,128)S(1)}, f32[128,896]{1,0:T(8,128)S(1)}, u32[]{:S(2)}, u32[]{:S(2)}) collective-permute-start(f32[128,896]{1,0:T(8,128)S(1)} %constant_dynamic-update-slice_fusion.refs_0_.refs_1_), channel_id=1, source_target_pairs={{0,1},{1,0},{2,3},{3,2},{4,5},{5,4},{6,7},{7,6},{8,9},{9,8},{10,11... | collective-permute-start | bytes 1376264 | tf_op jit(solution)/shard_map/ppermute | solution.py:383
  77.9 34.8 %all-to-all-start.3 = ((f32[64,24,256]{2,1,0:T(8,128)}), f32[64,24,256]{2,1,0:T(8,128)S(1)}, u32[]{:S(2)}, u32[]{:S(2)}) async-start(f32[64,24,256]{2,1,0:T(8,128)} %bitcast.26), calls=%async_computation.3 | async-start | bytes 3145728 | tf_op jit(solution)/shard_map/all_to_all | solution.py:390
  91.1 30.3 %copy-start.3 = (s32[96,1]{0,1:T(1,128)S(1)}, s32[96,1]{0,1:T(1,128)}, u32[]{:S(2)}) copy-start(s32[96,1]{0,1:T(1,128)} %param.10) | copy-start | bytes 1156
